TPU v7x, 32 devices: a whole 2x2x4 slice. The times are simulated.
32 devices in a mesh: space: 8 (over z, y), view: 4 (over x, core).
Axes of the slice: x: 2, y: 2, z: 4, core: 2. Of those that a mesh axis runs over, the one named last changes fastest.
Arguments:
- params: float32 [59, 16384], P(None, 'space'), may hold values from -8 to 514, as said below
- visible: int32 [8, 128, 16], P('space'), may hold values from 0 to 2047, as said below
- blocks: int32 [8, 128], P('space'), may hold values from 0 to 63, as said below
- counts: int32 [8, 8], P('space'), may hold values from 1 to 16
- depth_rank: int32 [4, 8], P('view'), may hold values from 0 to 7, each once within a row
- camera: float32 [4, 3], P('view'), may hold values from -0.006 to 0.006
- background: float32 [4, 3], P('view'), may hold values from 0 to 1
- target: float32 [4, 3, 128, 512], P('view', None, 'space'), may hold values from 0 to 1
Outputs:
- grad_params: float32 [59, 16384], P(None, 'space')
- rendered: float32 [4, 3, 128, 512], P('view', None, 'space')
- loss: float32 [4], P('view')
Inputs may be any that keep to these rules, and one draw needn't show every extreme that they name: `visible`: each row of a subspace's table lists 16 different splats of that subspace in increasing order; every splat of the subspace is listed exactly once. Slot j of a subspace goes to owner j // 16; the 16 slots that one subspace sends to one owner name different blocks. counts[s, o] live slots lead the 16 slots that subspace s sends to owner o. `params`: rows 6 to 9 of a column hold a quaternion whose first component lies in [1, 2].
All inputs are finite; a program needn't handle non-finite values.
Results may differ from a plain program's by a relative error of at most 0.0003.
Values sent between devices are 32-bit elements; how exact they have to be, the bound alone decides.
A program may use at most 64 MiB of HBM per device.

v0:
```python
import functools
import math

import jax
import jax.numpy as jnp
from jax import lax
from jax.experimental import pallas as pl
from jax.experimental.pallas import tpu as pltpu
from jax.sharding import PartitionSpec as P

HIGHEST = lax.Precision.HIGHEST
SH_ZERO = 0.28209479177387814
SH_ONE = 0.4886025119029199
SH_TWO = (
    1.0925484305920792,
    -1.0925484305920792,
    0.31539156525252005,
    -1.0925484305920792,
    0.5462742152960396,
)
SH_THREE = (
    -0.5900435899266435,
    2.890611442640554,
    -0.4570457994644658,
    0.3731763325901154,
    -0.4570457994644658,
    1.445305721320277,
    -0.5900435899266435,
)
DILATION = 0.3
SMOOTHING = 0.0001
SSIM_FIRST = 0.0001
SSIM_SECOND = 0.0009


def with_halo(x, sides, width):
    for axis, dim in sides:
        devices, length = (lax.axis_size(axis), x.shape[dim])
        up = [(i, (i + 1) % devices) for i in range(devices - 1)]
        down = [(j, i) for i, j in up]
        last = lax.slice_in_dim(x, length - width, length, axis=dim)
        first = lax.slice_in_dim(x, 0, width, axis=dim)
        before = lax.ppermute(last, axis, up)
        after = lax.ppermute(first, axis, down)
        x = jnp.concatenate([before, x, after], axis=dim)
    return x


def camera_rotation(angles):
    cos_a, sin_a = (jnp.cos(angles[0]), jnp.sin(angles[0]))
    cos_b, sin_b = (jnp.cos(angles[1]), jnp.sin(angles[1]))
    cos_c, sin_c = (jnp.cos(angles[2]), jnp.sin(angles[2]))
    return [
        [cos_c * cos_b, cos_c * sin_b * sin_a - sin_c * cos_a, cos_c * sin_b * cos_a + sin_c * sin_a],
        [sin_c * cos_b, sin_c * sin_b * sin_a + cos_c * cos_a, sin_c * sin_b * cos_a - cos_c * sin_a],
        [-sin_b, cos_b * sin_a, cos_b * cos_a],
    ]


def harmonics(view_axis):
    axis_x, axis_y, axis_z = (view_axis[0], view_axis[1], view_axis[2])
    sq_x, sq_y, sq_z = (axis_x * axis_x, axis_y * axis_y, axis_z * axis_z)
    return [
        SH_ZERO * jnp.ones_like(axis_x),
        -SH_ONE * axis_y,
        SH_ONE * axis_z,
        -SH_ONE * axis_x,
        SH_TWO[0] * axis_x * axis_y,
        SH_TWO[1] * axis_y * axis_z,
        SH_TWO[2] * (2.0 * sq_z - sq_x - sq_y),
        SH_TWO[3] * axis_x * axis_z,
        SH_TWO[4] * (sq_x - sq_y),
        SH_THREE[0] * axis_y * (3.0 * sq_x - sq_y),
        SH_THREE[1] * axis_x * axis_y * axis_z,
        SH_THREE[2] * axis_y * (4.0 * sq_z - sq_x - sq_y),
        SH_THREE[3] * axis_z * (2.0 * sq_z - 3.0 * sq_x - 3.0 * sq_y),
        SH_THREE[4] * axis_x * (4.0 * sq_z - sq_x - sq_y),
        SH_THREE[5] * axis_z * (sq_x - sq_y),
        SH_THREE[6] * axis_x * (sq_x - 3.0 * sq_y),
    ]


def geometry(rows, turns, centre_x, centre_y):
    scales = [jnp.exp(rows[i]) for i in range(3, 6)]
    quat = rows[6:10]
    length = jnp.sqrt(quat[0] * quat[0] + quat[1] * quat[1] + quat[2] * quat[2] + quat[3] * quat[3])
    part_w, part_x, part_y, part_z = [q / length for q in quat]
    spin = [
        [
            1.0 - 2.0 * (part_y * part_y + part_z * part_z),
            2.0 * (part_x * part_y - part_w * part_z),
            2.0 * (part_x * part_z + part_w * part_y),
        ],
        [
            2.0 * (part_x * part_y + part_w * part_z),
            1.0 - 2.0 * (part_x * part_x + part_z * part_z),
            2.0 * (part_y * part_z - part_w * part_x),
        ],
        [
            2.0 * (part_x * part_z - part_w * part_y),
            2.0 * (part_y * part_z + part_w * part_x),
            1.0 - 2.0 * (part_x * part_x + part_y * part_y),
        ],
    ]
    local = [[spin[r][c] * scales[c] for c in range(3)] for r in range(3)]
    opacity = 1.0 / (1.0 + jnp.exp(-rows[10]))
    shift_x = rows[0] - centre_x
    shift_y = rows[1] - centre_y
    records = []
    for turn in turns:
        frame = [
            [
                turn[r][0] * local[0][c] + turn[r][1] * local[1][c] + turn[r][2] * local[2][c]
                for c in range(3)
            ]
            for r in range(2)
        ]
        cov_xx = sum(frame[0][c] * frame[0][c] for c in range(3)) + DILATION
        cov_xy = sum(frame[0][c] * frame[1][c] for c in range(3))
        cov_yy = sum(frame[1][c] * frame[1][c] for c in range(3)) + DILATION
        inverse = 1.0 / (cov_xx * cov_yy - cov_xy * cov_xy)
        mean_u = turn[0][0] * shift_x + turn[0][1] * shift_y + turn[0][2] * rows[2] + centre_x
        mean_w = turn[1][0] * shift_x + turn[1][1] * shift_y + turn[1][2] * rows[2] + centre_y
        records.append(
            [mean_u, mean_w, cov_yy * inverse, -cov_xy * inverse, cov_xx * inverse, opacity]
        )
    return records


def split_parts(value):
    high = value.astype(jnp.bfloat16)
    rest = value - high.astype(jnp.float32)
    middle = rest.astype(jnp.bfloat16)
    low = (rest - middle.astype(jnp.float32)).astype(jnp.bfloat16)
    return jnp.concatenate([high, middle, low], axis=0)


def chunk_of(total):
    return 256 if total % 256 == 0 else total


def one_hot(lists_ref, start, chunk, splats):
    wanted = lists_ref[:, pl.ds(start, chunk)]
    rows = lax.broadcasted_iota(jnp.int32, (splats, chunk), 0)
    return jnp.where(rows == wanted, 1.0, 0.0).astype(jnp.bfloat16)


def project_kernel(centre_x, centre_y, params_ref, lists_ref, camera_ref, extra_ref, out_ref, rec_ref, parts_ref):
    splats = params_ref.shape[1]
    total = lists_ref.shape[1]
    turn = camera_rotation([camera_ref[:, i : i + 1] for i in range(3)])
    rows = [params_ref[i : i + 1, :] for i in range(11)]
    record = geometry(rows, [turn], centre_x, centre_y)[0]
    basis = harmonics(turn[2])
    colour = 0.5 + basis[0] * params_ref[11:14, :]
    for i in range(1, 16):
        colour = colour + basis[i] * params_ref[11 + 3 * i : 14 + 3 * i, :]
    rec_ref[...] = jnp.zeros_like(rec_ref)
    for i in range(6):
        rec_ref[i : i + 1, :] = record[i]
    rec_ref[6:9, :] = colour
    parts_ref[...] = split_parts(rec_ref[...])
    chunk = chunk_of(total)

    def step(index, carry):
        start = pl.multiple_of(index * chunk, chunk)
        picked = jnp.dot(
            parts_ref[...],
            one_hot(lists_ref, start, chunk, splats),
            preferred_element_type=jnp.float32,
        )
        out_ref[:, pl.ds(start, chunk)] = picked[0:16] + picked[16:32] + picked[32:48]
        return carry

    lax.fori_loop(0, total // chunk, step, 0)
    out_ref[9:10, :] = extra_ref[...]


def unpick_kernel(grads_ref, lists_ref, camera_ref, out_ref, acc_ref):
    splats = out_ref.shape[1]
    total = lists_ref.shape[1]
    chunk = chunk_of(total)
    acc_ref[...] = jnp.zeros_like(acc_ref)

    def step(index, carry):
        start = pl.multiple_of(index * chunk, chunk)
        acc_ref[...] += lax.dot_general(
            split_parts(grads_ref[:, pl.ds(start, chunk)]),
            one_hot(lists_ref, start, chunk, splats),
            (((1,), (1,)), ((), ())),
            preferred_element_type=jnp.float32,
        )
        return carry

    lax.fori_loop(0, total // chunk, step, 0)
    out_ref[...] = acc_ref[0:16, :] + acc_ref[16:32, :] + acc_ref[32:48, :]
    for i in range(3):
        out_ref[9 + i : 10 + i, :] = jnp.broadcast_to(camera_ref[:, i : i + 1], (1, splats))


def unproject_kernel(centre_x, centre_y, params_ref, grads_ref, out_ref):
    views = grads_ref.shape[0]
    turns = [
        camera_rotation([grads_ref[v, 9 + i : 10 + i, 0:1] for i in range(3)]) for v in range(views)
    ]
    rows = [params_ref[i : i + 1, :] for i in range(11)]
    pull = jax.vjp(lambda r: geometry(r, turns, centre_x, centre_y), rows)[1]
    cotangents = [[grads_ref[v, i : i + 1, :] for i in range(6)] for v in range(views)]
    for i, value in enumerate(pull(cotangents)[0]):
        out_ref[i : i + 1, :] = value
    bases = [harmonics(turn[2]) for turn in turns]
    colours = [grads_ref[v, 6:9, :] for v in range(views)]
    for i in range(16):
        value = bases[0][i] * colours[0]
        for v in range(1, views):
            value = value + bases[v][i] * colours[v]
        out_ref[11 + 3 * i : 14 + 3 * i, :] = value


def whole_call(kernel, name, shape, scratch, *args):
    return pl.pallas_call(
        kernel,
        name=name,
        out_shape=jax.ShapeDtypeStruct(shape, jnp.float32),
        in_specs=[pl.BlockSpec(memory_space=pltpu.VMEM)] * len(args),
        out_specs=pl.BlockSpec(memory_space=pltpu.VMEM),
        scratch_shapes=scratch,
    )(*args)


def render(gathered, grid_x, grid_y):
    delta_x = grid_x[:, None, :] - gathered[0][:, :, None]
    delta_y = grid_y[:, None, :] - gathered[1][:, :, None]
    powers = 0.5 * (
        gathered[2][:, :, None] * delta_x * delta_x
        + 2.0 * gathered[3][:, :, None] * delta_x * delta_y
        + gathered[4][:, :, None] * delta_y * delta_y
    )
    alphas = gathered[5][:, :, None] * jnp.exp(-powers)
    kept_log = jnp.log1p(-alphas)
    before = jnp.cumsum(kept_log, axis=1) - kept_log
    weights = alphas * jnp.exp(before)
    colour = jnp.einsum("skp,csk->scp", weights, gathered[6:9], precision=HIGHEST)
    return jnp.concatenate([colour, jnp.sum(kept_log, axis=1)[:, None, :]], axis=1)


def pixel_grid(owners, blocks_used, strip_rows, block_cols):
    inner = jnp.arange(128, dtype=jnp.int32)
    corner_y = owners * strip_rows + blocks_used // block_cols * 8
    corner_x = blocks_used % block_cols * 16
    grid_y = (corner_y[:, None] + inner[None, :] // 16).astype(jnp.float32) + 0.5
    grid_x = (corner_x[:, None] + inner[None, :] % 16).astype(jnp.float32) + 0.5
    return (grid_x, grid_y)


def composite(pieces, target_ids, depth_ranks, backdrop, block_rows, block_cols):
    block_count = block_rows * block_cols
    onehot = (
        target_ids[:, :, None] == jnp.arange(block_count, dtype=jnp.int32)[None, None, :]
    ).astype(jnp.float32)
    dense = jnp.einsum("scb,scqp->bsqp", onehot, pieces, precision=HIGHEST)
    kept_log = dense[:, :, 3]
    nearer = (depth_ranks[None, :] < depth_ranks[:, None]).astype(jnp.float32)
    before = jnp.einsum("st,btp->bsp", nearer, kept_log, precision=HIGHEST)
    picture = jnp.einsum("bsp,bscp->bcp", jnp.exp(before), dense[:, :, 0:3], precision=HIGHEST)
    picture = picture + backdrop[None, :, None] * jnp.exp(jnp.sum(kept_log, axis=1))[:, None, :]
    picture = picture.reshape(block_rows, block_cols, 3, 8, 16).transpose(2, 0, 3, 1, 4)
    return picture.reshape(3, block_rows * 8, block_cols * 16)


def blur_taps():
    raw_taps = [math.exp(-(offset - 5) * (offset - 5) / 4.5) for offset in range(11)]
    total = sum(raw_taps)
    return [value / total for value in raw_taps]


def blur(values, count):
    taps = blur_taps()
    width_px = values.shape[2]
    padded = jnp.pad(values, ((0, 0), (0, 0), (5, 5)))
    across = taps[0] * padded[:, :, 0:width_px]
    for offset in range(1, 11):
        across = across + taps[offset] * padded[:, :, offset : offset + width_px]
    result = taps[0] * across[:, 0:count]
    for offset in range(1, 11):
        result = result + taps[offset] * across[:, offset : offset + count]
    return result


def pixel_terms(picture, goal, count):
    mean_a = blur(picture, count)
    mean_b = blur(goal, count)
    var_a = blur(picture * picture, count) - mean_a * mean_a
    var_b = blur(goal * goal, count) - mean_b * mean_b
    cov_ab = blur(picture * goal, count) - mean_a * mean_b
    ssim = (
        (2.0 * mean_a * mean_b + SSIM_FIRST)
        * (2.0 * cov_ab + SSIM_SECOND)
        / ((mean_a * mean_a + mean_b * mean_b + SSIM_FIRST) * (var_a + var_b + SSIM_SECOND))
    )
    differ = picture[:, 5 : 5 + count] - goal[:, 5 : 5 + count]
    return 0.8 * jnp.sqrt(differ * differ + SMOOTHING) + 0.2 * (1.0 - ssim)


def shards(params, visible, blocks, counts, depth_rank, camera, background, target):
    devices = lax.axis_size("space")
    me_index = lax.axis_index("space")
    slot_total = visible.shape[1]
    list_length = visible.shape[2]
    capacity = slot_total // devices
    strip_rows = target.shape[2]
    width_px = target.shape[3]
    block_rows = strip_rows // 8
    block_cols = width_px // 16
    height_px = strip_rows * devices
    splats = params.shape[1]
    lists = visible[0].reshape(1, slot_total * list_length)
    live = jnp.arange(capacity, dtype=jnp.int32)[None, :] < counts[0][:, None]
    target_ids = jnp.where(live, blocks[0].reshape(devices, capacity), -1).astype(jnp.float32)
    id_row = jnp.broadcast_to(target_ids[:, :, None], (devices, capacity, list_length))
    centre_x = 0.5 * width_px
    centre_y = 0.5 * height_px
    message = whole_call(
        functools.partial(project_kernel, centre_x, centre_y),
        "project",
        (16, slot_total * list_length),
        [pltpu.VMEM((16, splats), jnp.float32), pltpu.VMEM((48, splats), jnp.bfloat16)],
        params,
        lists,
        camera,
        id_row.reshape(1, slot_total * list_length),
    )
    message = message[0:10].reshape(10, devices, capacity * list_length).transpose(1, 0, 2)
    received = lax.all_to_all(message, "space", split_axis=0, concat_axis=0, tiled=True)
    recv_ids = received[:, 9].reshape(devices, capacity, list_length)[:, :, 0].astype(jnp.int32)
    own_blocks = jnp.maximum(recv_ids.reshape(devices * capacity), 0)
    grid_x, grid_y = pixel_grid(
        jnp.full(own_blocks.shape, me_index, jnp.int32), own_blocks, strip_rows, block_cols
    )

    def owner_side(recv_in):
        gathered = (
            recv_in.reshape(devices, 9, capacity, list_length)
            .transpose(1, 0, 2, 3)
            .reshape(9, devices * capacity, list_length)
        )
        pieces = render(gathered, grid_x, grid_y).reshape(devices, capacity, 4, 128)
        return composite(pieces, recv_ids, depth_rank[0], background[0], block_rows, block_cols)

    strip, pull_owner = jax.vjp(owner_side, received[:, 0:9])
    stacked = jnp.concatenate([strip, target[0]], axis=0)
    extended = with_halo(stacked, (("space", 1),), 10)
    goal = extended[3:6]
    rows_here = strip_rows + 10
    terms, pull_terms = jax.vjp(lambda p: pixel_terms(p, goal, rows_here), extended[0:3])
    own_loss = jnp.sum(terms[:, 5 : 5 + strip_rows])
    row_ids = jnp.arange(rows_here, dtype=jnp.int32) + me_index * strip_rows - 5
    inside = ((row_ids >= 0) & (row_ids < height_px)).astype(jnp.float32)
    ones = jnp.broadcast_to(inside[None, :, None], terms.shape)
    grad_strip = pull_terms(ones)[0][:, 10 : 10 + strip_rows]
    grad_received = pull_owner(grad_strip)[0]
    loss_row = jnp.broadcast_to(own_loss, (devices, 1, capacity * list_length))
    returned = lax.all_to_all(
        jnp.concatenate([grad_received, loss_row], axis=1),
        "space",
        split_axis=0,
        concat_axis=0,
        tiled=True,
    )
    loss_sum = jnp.sum(returned[:, 9, 0])
    grad_slots = returned.transpose(1, 0, 2).reshape(10, slot_total * list_length)
    grad_slots = jnp.pad(grad_slots[0:9], ((0, 7), (0, 0)))
    grad_records = whole_call(
        unpick_kernel,
        "unpick",
        (16, splats),
        [pltpu.VMEM((48, splats), jnp.float32)],
        grad_slots,
        lists,
        camera,
    )
    every_view = lax.all_gather(grad_records, "view", axis=0, tiled=False)
    grad_params = whole_call(
        functools.partial(unproject_kernel, centre_x, centre_y),
        "unproject",
        params.shape,
        [],
        params,
        every_view,
    )
    loss_value = (loss_sum / (3.0 * height_px * width_px)).reshape(1)
    return (grad_params, strip[None], loss_value)


def solution(mesh):
    in_specs = (
        P(None, "space"),
        P("space", None, None),
        P("space", None),
        P("space", None),
        P("view", None),
        P("view", None),
        P("view", None),
        P("view", None, "space", None),
    )
    out_specs = (P(None, "space"), P("view", None, "space", None), P("view"))
    return jax.shard_map(shards, mesh=mesh, in_specs=in_specs, out_specs=out_specs, check_vma=False)
```

profile of v0, /device:TPU:0, one launch (start us, length us, event | category | flops | bytes accessed | tf_op | source)
XLA Modules:
  0.0 113.9 jit_solution(12949749248739057759)
XLA Ops:
  4.3 4.4 %project.1 = f32[16,2048]{1,0:T(8,128)} custom-call(f32[59,2048]{1,0:T(8,128)} %params_ref.3, s32[1,2048]{1,0:T(1,128)} %reshape_squeeze.9.lists_ref, f32[1,3]{1,0:T(1,128)} %camera_ref.3, f32[1,2048]{1,0:T(1,128)} %reshape.318.extra_ref), custom_call_target="tpu_custom_call" | custom-call | tf_op jit(solution)/shard_map/project/pallas_call | solution.py:221
  8.7 0.9 copy.130
  10.4 7.3 %all-to-all-start = ((f32[8,10,256]{2,1,0:T(8,128)}), f32[8,10,256]{2,1,0:T(8,128)S(1)}, u32[]{:S(2)}, u32[]{:S(2)}) async-start(f32[8,10,256]{2,1,0:T(8,128)} %bitcast.96), calls=%async_computation | async-start | bytes 262144 | tf_op jit(solution)/shard_map/all_to_all | solution.py:334
  17.7 7.3 %all-to-all-done = f32[8,10,256]{2,1,0:T(8,128)S(1)} async-done(((f32[8,10,256]{2,1,0:T(8,128)}), f32[8,10,256]{2,1,0:T(8,128)S(1)}, u32[]{:S(2)}, u32[]{:S(2)}) %all-to-all-start) | async-done | bytes 81952 | tf_op jit(solution)/shard_map/all_to_all | solution.py:334
  26.8 1.7 %negate_log-plus-one_fusion = (f32[128,16,128]{2,1,0:T(8,128)S(1)}, f32[128,128]{1,0:T(8,128)S(1)}) fusion(f32[128,16]{1,0:T(8,128)S(1)} %bitcast.110, f32[128,16]{1,0:T(8,128)S(1)} %bitcast.115, f32[128,16]{1,0:T(8,128)S(1)} %bitcast.120, f32[128,128]{1,0:T(8,128)S(1)} %get-tuple-element.85, f32[128,16]{1,0:T(8,128)S(1)} %bitcast.125, ...), kind=kLoop, calls=%fused_computation.50 | loop fusion | flops 3915776 | bytes 1294336 | tf_op jit(solution)/shard_map/jvp()/log1p | solution.py:240
  29.0 3.7 %fusion.28 = f32[128,3,128]{2,1,0:T(4,128)S(1)} fusion(f32[3,128,16]{2,0,1:T(4,128)S(1)} %bitcast.152, f32[128,16]{1,0:T(8,128)S(1)} %bitcast.111, f32[128,16,128]{2,0,1:T(8,128)S(1)} %fusion.26, f32[128,16]{1,0:T(8,128)S(1)} %bitcast.116, f32[128,16]{1,0:T(8,128)S(1)} %bitcast.121, f32[128,128]{1,0:T(8,128)S(1)} %get-tuple-element.85, ...), kind=kOutput, calls=%fused_computation.108 | convolution fusion | flops 13631488 | bytes 1449984 | tf_op jit(solution)/shard_map/jvp(skp,csk->scp)/dot_general | solution.py:243
  32.7 0.7 convolution_bitcast_fusion
  37.8 2.1 %collective-permute-start = (f32[6,10,512]{2,1,0:T(8,128)S(1)}, f32[6,10,512]{2,1,0:T(8,128)S(1)}, u32[]{:S(2)}, u32[]{:S(2)}) collective-permute-start(f32[6,10,512]{2,1,0:T(8,128)S(1)} %get-tuple-element.79), channel_id=1, source_target_pairs={{0,4},{4,8},{8,12},{12,16},{16,20},{20,24},{24,28},{1,5},{5,9},{9,... | collective-permute-start | bytes 368648 | tf_op jit(solution)/shard_map/ppermute | solution.py:43
  40.0 1.5 %collective-permute-start.1 = (f32[6,10,512]{2,1,0:T(8,128)S(1)}, f32[6,10,512]{2,1,0:T(8,128)S(1)}, u32[]{:S(2)}, u32[]{:S(2)}) collective-permute-start(f32[6,10,512]{2,1,0:T(8,128)S(1)} %get-tuple-element.80), channel_id=1, source_target_pairs={{4,0},{8,4},{12,8},{16,12},{20,16},{24,20},{28,24},{5,1},{9,5},{13... | collective-permute-start | bytes 368648 | tf_op jit(solution)/shard_map/ppermute | solution.py:44
  41.5 5.9 %collective-permute-done = f32[6,10,512]{2,1,0:T(8,128)S(1)} collective-permute-done((f32[6,10,512]{2,1,0:T(8,128)S(1)}, f32[6,10,512]{2,1,0:T(8,128)S(1)}, u32[]{:S(2)}, u32[]{:S(2)}) %collective-permute-start) | collective-permute-done | bytes 122912 | tf_op jit(solution)/shard_map/ppermute | solution.py:43
  47.7 0.8 add_sqrt_fusion
  52.1 1.4 %fusion.209 = (f32[3,26,512]{2,1,0:T(8,128)}, f32[3,26,512]{2,1,0:T(8,128)S(1)}, f32[3,26,512]{2,1,0:T(8,128)S(1)}, f32[3,26,512]{2,1,0:T(8,128)S(1)}) fusion(f32[3,36,512]{2,1,0:T(8,128)S(1)} %fusion.129, f32[3,36,512]{2,1,0:T(8,128)S(1)} %fusion.69, f32[3,36,512]{2,1,0:T(8,128)S(1)} %fusion.49), kind=kLoop, calls=%fused_computation.431 | loop fusion | flops 2835456 | bytes 5910528 | tf_op jit(solution)/shard_map/jvp()/mul | solution.py:297
  53.5 1.2 %fusion.212 = (f32[3,26,512]{2,1,0:T(8,128)}, f32[3,26,512]{2,1,0:T(8,128)S(1)}) fusion(f32[3,26,512]{2,1,0:T(8,128)S(1)} %get-tuple-element.14, f32[3,26,512]{2,1,0:T(8,128)S(1)} %get-tuple-element.15, f32[3,36,512]{2,1,0:T(8,128)S(1)} %fusion.109, f32[3,36,512]{2,1,0:T(8,128)S(1)} %fusion.89), kind=kLoop, calls=%fused_computation.434 | loop fusion | flops 2036736 | bytes 4153344 | tf_op jit(solution)/shard_map/jvp()/mul | solution.py:299
  63.6 4.4 %convolution_bitcast_fusion.1 = f32[3,128,16]{2,0,1:T(4,128)S(1)} fusion(f32[128,16]{1,0:T(8,128)S(1)} %bitcast.112, f32[128,16,128]{2,0,1:T(8,128)S(1)} %copy-done.1, f32[128,3,128]{2,0,1:T(8,128)S(1)} %split.8, f32[128,16]{1,0:T(8,128)S(1)} %bitcast.117, f32[128,16]{1,0:T(8,128)S(1)} %bitcast.122, f32[128,128]{1,0:T(8,128)S(1)} %copy-done.15, ...), kind=kOutput, calls=%fused_computation.16 | convolution fusion | flops 13631488 | bytes 1449984 | tf_op jit(solution)/shard_map/transpose(jvp(skp,csk->scp))/dot_general | solution.py:243
  68.0 4.0 %multiply_multiply_fusion = (f32[128,16,128]{2,1,0:T(8,128)S(1)}, f32[128,16,128]{2,1,0:T(8,128)S(1)}) fusion(f32[128,16]{1,0:T(8,128)S(1)} %bitcast.113, f32[128,16,128]{2,0,1:T(8,128)S(1)} %copy-done.1, f32[128,16]{1,0:T(8,128)S(1)} %bitcast.118, f32[128,16]{1,0:T(8,128)S(1)} %bitcast.123, f32[128,128]{1,0:T(8,128)S(1)} %copy-done.15, ...), kind=kOutput, calls=%fused_computation.48 | convolution fusion | flops 13893632 | bytes 3547136 | tf_op jit(solution)/shard_map/transpose(jvp(skp,csk->scp))/dot_general | solution.py:243
  72.3 5.6 %fusion.15 = (f32[128,16]{1,0:T(8,128)S(1)}, f32[128,16]{1,0:T(8,128)S(1)}, f32[128,16]{1,0:T(8,128)S(1)}, f32[128,16]{1,0:T(8,128)S(1)}, f32[128,16]{1,0:T(8,128)S(1)}, /*index=5*/f32[128,16]{1,0:T(8,128)S(1)}) fusion(f32[128,16]{1,0:T(8,128)S(1)} %bitcast.124, f32[128,128]{1,0:T(8,128)S(1)} %copy-done.15, f32[128,16]{1,0:T(8,128)S(1)} %bitcast.119, ...), kind=kLoop, calls=%fused_computation.30 | loop fusion | flops 13357056 | bytes 3440640 | tf_op jit(solution)/shard_map/transpose(jvp())/reduce_sum | solution.py:237
  77.9 0.9 pad_add_fusion
  80.9 1.3 %concatenate.22.clone = f32[8,10,256]{2,1,0:T(8,128)} pad(f32[8,9,256]{2,1,0:T(8,128)S(1)} %copy.128, f32[]{:T(128)} %fusion.200), padding=0_0x0_1x0_0 | pad | bytes 155652 | tf_op jit(solution)/shard_map/concatenate | solution.py:364
  82.2 4.7 %all-to-all-start.1 = ((f32[8,10,256]{2,1,0:T(8,128)}), f32[8,10,256]{2,1,0:T(8,128)S(1)}, u32[]{:S(2)}, u32[]{:S(2)}) async-start(f32[8,10,256]{2,1,0:T(8,128)} %concatenate.22.clone), calls=%async_computation.1 | async-start | bytes 262144 | tf_op jit(solution)/shard_map/all_to_all | solution.py:363
  86.9 1.0 reshape.328
  87.9 6.3 %all-to-all-done.1 = f32[8,10,256]{2,1,0:T(8,128)S(1)} async-done(((f32[8,10,256]{2,1,0:T(8,128)}), f32[8,10,256]{2,1,0:T(8,128)S(1)}, u32[]{:S(2)}, u32[]{:S(2)}) %all-to-all-start.1) | async-done | bytes 81952 | tf_op jit(solution)/shard_map/all_to_all | solution.py:363
  95.0 5.1 %unpick.1 = f32[16,2048]{1,0:T(8,128)} custom-call(f32[16,2048]{1,0:T(8,128)} %pad.347.grads_ref, s32[1,2048]{1,0:T(1,128)} %reshape_squeeze.9.lists_ref, f32[1,3]{1,0:T(1,128)} %camera_ref.3), custom_call_target="tpu_custom_call" | custom-call | tf_op jit(solution)/shard_map/unpick/pallas_call | solution.py:221
  100.1 8.1 %all-gather = f32[64,2048]{1,0:T(8,128)} all-gather(f32[16,2048]{1,0:T(8,128)} %unpick.1), channel_id=2, replica_groups=mesh['space'=8,'view'=4] {'view'}, dimensions={0}, use_global_device_ids=true | all-gather | bytes 655360 | tf_op jit(solution)/shard_map/all_gather | solution.py:382
  108.3 3.3 %unproject.1 = f32[59,2048]{1,0:T(8,128)} custom-call(f32[59,2048]{1,0:T(8,128)} %params_ref.3, f32[4,16,2048]{2,1,0:T(8,128)} %bitcast.105), custom_call_target="tpu_custom_call" | custom-call | tf_op jit(solution)/shard_map/unproject/pallas_call | solution.py:221
  (157 shorter events, 27.0 us)
Async XLA Ops:
  10.4 14.7 %all-to-all-start = ((f32[8,10,256]{2,1,0:T(8,128)}), f32[8,10,256]{2,1,0:T(8,128)S(1)}, u32[]{:S(2)}, u32[]{:S(2)}) async-start(f32[8,10,256]{2,1,0:T(8,128)} %bitcast.96), calls=%async_computation | async-start | bytes 262144 | tf_op jit(solution)/shard_map/all_to_all | solution.py:334
  26.2 2.7 %copy-start.2 = (f32[1,8,16,16]{3,2,1,0:T(8,128)}, f32[1,8,16,16]{3,2,1,0:T(8,128)S(1)}, u32[]{:S(2)}) copy-start(f32[1,8,16,16]{3,2,1,0:T(8,128)S(1)} %get-tuple-element.34) | copy-start | bytes 24580
  26.2 2.7 %copy-start.4 = (f32[1,8,16,16]{3,2,1,0:T(8,128)}, f32[1,8,16,16]{3,2,1,0:T(8,128)S(1)}, u32[]{:S(2)}) copy-start(f32[1,8,16,16]{3,2,1,0:T(8,128)S(1)} %get-tuple-element.35) | copy-start | bytes 24580
  26.2 2.7 %copy-start.6 = (f32[1,8,16,16]{3,2,1,0:T(8,128)}, f32[1,8,16,16]{3,2,1,0:T(8,128)S(1)}, u32[]{:S(2)}) copy-start(f32[1,8,16,16]{3,2,1,0:T(8,128)S(1)} %get-tuple-element.36) | copy-start | bytes 24580
  26.2 2.7 %copy-start.8 = (f32[1,8,16,16]{3,2,1,0:T(8,128)}, f32[1,8,16,16]{3,2,1,0:T(8,128)S(1)}, u32[]{:S(2)}) copy-start(f32[1,8,16,16]{3,2,1,0:T(8,128)S(1)} %get-tuple-element.37) | copy-start | bytes 24580
  26.2 2.7 %copy-start.10 = (f32[1,8,16,16]{3,2,1,0:T(8,128)}, f32[1,8,16,16]{3,2,1,0:T(8,128)S(1)}, u32[]{:S(2)}) copy-start(f32[1,8,16,16]{3,2,1,0:T(8,128)S(1)} %get-tuple-element.38) | copy-start | bytes 24580
  26.2 2.7 %copy-start.12 = (f32[1,8,16,16]{3,2,1,0:T(8,128)}, f32[1,8,16,16]{3,2,1,0:T(8,128)S(1)}, u32[]{:S(2)}) copy-start(f32[1,8,16,16]{3,2,1,0:T(8,128)S(1)} %get-tuple-element.39) | copy-start | bytes 24580
  26.6 2.3 %copy-start.24 = (f32[3,8,16,16]{3,0,2,1:T(4,128)}, f32[3,8,16,16]{3,0,2,1:T(4,128)S(1)}, u32[]{:S(2)}) copy-start(f32[3,8,16,16]{3,0,2,1:T(4,128)S(1)} %copy.84) | copy-start | bytes 73732
  26.8 2.2 %copy-start.14 = (f32[128,128]{1,0:T(8,128)}, f32[128,128]{1,0:T(8,128)S(1)}, u32[]{:S(2)}) copy-start(f32[128,128]{1,0:T(8,128)S(1)} %get-tuple-element.85) | copy-start | bytes 196612
  26.8 2.2 %copy-start.16 = (f32[128,128]{1,0:T(8,128)}, f32[128,128]{1,0:T(8,128)S(1)}, u32[]{:S(2)}) copy-start(f32[128,128]{1,0:T(8,128)S(1)} %get-tuple-element.86) | copy-start | bytes 196612
  28.9 3.8 %copy-start = (f32[128,16,128]{2,0,1:T(8,128)}, f32[128,16,128]{2,0,1:T(8,128)S(1)}, u32[]{:S(2)}) copy-start(f32[128,16,128]{2,0,1:T(8,128)S(1)} %fusion.26) | copy-start | bytes 3145732
  37.8 9.5 %collective-permute-start = (f32[6,10,512]{2,1,0:T(8,128)S(1)}, f32[6,10,512]{2,1,0:T(8,128)S(1)}, u32[]{:S(2)}, u32[]{:S(2)}) collective-permute-start(f32[6,10,512]{2,1,0:T(8,128)S(1)} %get-tuple-element.79), channel_id=1, source_target_pairs={{0,4},{4,8},{8,12},{12,16},{16,20},{20,24},{24,28},{1,5},{5,9},{9,... | collective-permute-start | bytes 368648 | tf_op jit(solution)/shard_map/ppermute | solution.py:43
  40.0 7.6 %collective-permute-start.1 = (f32[6,10,512]{2,1,0:T(8,128)S(1)}, f32[6,10,512]{2,1,0:T(8,128)S(1)}, u32[]{:S(2)}, u32[]{:S(2)}) collective-permute-start(f32[6,10,512]{2,1,0:T(8,128)S(1)} %get-tuple-element.80), channel_id=1, source_target_pairs={{4,0},{8,4},{12,8},{16,12},{20,16},{24,20},{28,24},{5,1},{9,5},{13... | collective-permute-start | bytes 368648 | tf_op jit(solution)/shard_map/ppermute | solution.py:44
  61.9 1.2 %copy-start.1 = (f32[128,16,128]{2,0,1:T(8,128)S(1)}, f32[128,16,128]{2,0,1:T(8,128)}, u32[]{:S(2)}) copy-start(f32[128,16,128]{2,0,1:T(8,128)} %copy-done) | copy-start | bytes 3145732
  62.5 0.9 copy-start.17
  62.5 0.9 copy-start.5
  62.6 0.9 copy-start.7
  62.6 0.9 copy-start.9
  62.6 1.0 copy-start.11
  62.6 1.0 copy-start.13
  63.6 4.4 %copy-start.25 = (f32[3,8,16,16]{3,0,2,1:T(4,128)S(1)}, f32[3,8,16,16]{3,0,2,1:T(4,128)}, u32[]{:S(2)}) copy-start(f32[3,8,16,16]{3,0,2,1:T(4,128)} %copy-done.24) | copy-start | bytes 73732
  79.0 1.0 copy-start.20
  79.3 1.0 copy-start.18
  82.2 12.0 %all-to-all-start.1 = ((f32[8,10,256]{2,1,0:T(8,128)}), f32[8,10,256]{2,1,0:T(8,128)S(1)}, u32[]{:S(2)}, u32[]{:S(2)}) async-start(f32[8,10,256]{2,1,0:T(8,128)} %concatenate.22.clone), calls=%async_computation.1 | async-start | bytes 262144 | tf_op jit(solution)/shard_map/all_to_all | solution.py:363
  (11 other events, 8.4 us)
where the time goes:
time: 115 us; the launch traced here: 114 us
  other arithmetic  23.9 us (21%)
  waiting for transfers between devices  19.7 us (17%)
  local copies, waits for them, and re-layouts  16.5 us (14%)
  starting transfers between devices  15.6 us (14%)
  matrix products  14.2 us (12%)
  Pallas kernels  12.8 us (11%)
  blocking collectives  8.15 us (7%)
  between operations  3.24 us (3%)
    pallas_call x3, Pallas kernels, whole_call(): pl.pallas_call(kernel, name=name, out_shape=jax.ShapeDtypeStruct(shape, j...  12.8 us
    dot_general x3, matrix products, render(): jnp.einsum('skp,csk->scp', weights, gathered[6:9], precision=HIGHEST)  12 us
    all_gather x1, blocking collectives, shards(): every_view = lax.all_gather(grad_records, 'view', axis=0, tiled=False)  8.15 us
    unnamed x69, local copies, waits for them, and re-layouts  7.52 us
    all_to_all x1, waiting for transfers between devices, shards(): lax.all_to_all(message, 'space', split_axis=0, concat_axis=0, tiled=True)  7.32 us
    all_to_all x1, starting transfers between devices, shards(): lax.all_to_all(message, 'space', split_axis=0, concat_axis=0, tiled=True)  7.31 us
    all_to_all x1, waiting for transfers between devices, shards(): lax.all_to_all(jnp.concatenate([grad_received, loss_row], axis=1), 'space...  6.3 us
    ppermute x1, waiting for transfers between devices, with_halo(): before = lax.ppermute(last, axis, up)  5.9 us
  transfers between devices with their start and end apart: 4, of which 4 were waited for; matrix products, arithmetic and copies ran while one was open for 1% of the time, Pallas kernels for 0%

commit v1 on v0

v1 whole, which is shorter than its diff:
```python
import functools
import math

import jax
import jax.numpy as jnp
from jax import lax
from jax.experimental import pallas as pl
from jax.experimental.pallas import tpu as pltpu
from jax.sharding import PartitionSpec as P

F32 = jnp.float32
BF16 = jnp.bfloat16
I32 = jnp.int32
LANES = 128
LOG2E = 1.4426950408889634
SH_ZERO = 0.28209479177387814
SH_ONE = 0.4886025119029199
SH_TWO = (
    1.0925484305920792,
    -1.0925484305920792,
    0.31539156525252005,
    -1.0925484305920792,
    0.5462742152960396,
)
SH_THREE = (
    -0.5900435899266435,
    2.890611442640554,
    -0.4570457994644658,
    0.3731763325901154,
    -0.4570457994644658,
    1.445305721320277,
    -0.5900435899266435,
)
DILATION = 0.3
SMOOTHING = 0.0001
SSIM_FIRST = 0.0001
SSIM_SECOND = 0.0009


def camera_rotation(angles):
    cos_a, sin_a = (jnp.cos(angles[0]), jnp.sin(angles[0]))
    cos_b, sin_b = (jnp.cos(angles[1]), jnp.sin(angles[1]))
    cos_c, sin_c = (jnp.cos(angles[2]), jnp.sin(angles[2]))
    return [
        [cos_c * cos_b, cos_c * sin_b * sin_a - sin_c * cos_a, cos_c * sin_b * cos_a + sin_c * sin_a],
        [sin_c * cos_b, sin_c * sin_b * sin_a + cos_c * cos_a, sin_c * sin_b * cos_a - cos_c * sin_a],
        [-sin_b, cos_b * sin_a, cos_b * cos_a],
    ]


def harmonics(view_axis):
    axis_x, axis_y, axis_z = (view_axis[0], view_axis[1], view_axis[2])
    sq_x, sq_y, sq_z = (axis_x * axis_x, axis_y * axis_y, axis_z * axis_z)
    return [
        SH_ZERO * jnp.ones_like(axis_x),
        -SH_ONE * axis_y,
        SH_ONE * axis_z,
        -SH_ONE * axis_x,
        SH_TWO[0] * axis_x * axis_y,
        SH_TWO[1] * axis_y * axis_z,
        SH_TWO[2] * (2.0 * sq_z - sq_x - sq_y),
        SH_TWO[3] * axis_x * axis_z,
        SH_TWO[4] * (sq_x - sq_y),
        SH_THREE[0] * axis_y * (3.0 * sq_x - sq_y),
        SH_THREE[1] * axis_x * axis_y * axis_z,
        SH_THREE[2] * axis_y * (4.0 * sq_z - sq_x - sq_y),
        SH_THREE[3] * axis_z * (2.0 * sq_z - 3.0 * sq_x - 3.0 * sq_y),
        SH_THREE[4] * axis_x * (4.0 * sq_z - sq_x - sq_y),
        SH_THREE[5] * axis_z * (sq_x - sq_y),
        SH_THREE[6] * axis_x * (sq_x - 3.0 * sq_y),
    ]


def geometry(rows, turns, centre_x, centre_y):
    scales = [jnp.exp(rows[i]) for i in range(3, 6)]
    quat = rows[6:10]
    length = jnp.sqrt(quat[0] * quat[0] + quat[1] * quat[1] + quat[2] * quat[2] + quat[3] * quat[3])
    part_w, part_x, part_y, part_z = [q / length for q in quat]
    spin = [
        [
            1.0 - 2.0 * (part_y * part_y + part_z * part_z),
            2.0 * (part_x * part_y - part_w * part_z),
            2.0 * (part_x * part_z + part_w * part_y),
        ],
        [
            2.0 * (part_x * part_y + part_w * part_z),
            1.0 - 2.0 * (part_x * part_x + part_z * part_z),
            2.0 * (part_y * part_z - part_w * part_x),
        ],
        [
            2.0 * (part_x * part_z - part_w * part_y),
            2.0 * (part_y * part_z + part_w * part_x),
            1.0 - 2.0 * (part_x * part_x + part_y * part_y),
        ],
    ]
    local = [[spin[r][c] * scales[c] for c in range(3)] for r in range(3)]
    opacity = 1.0 / (1.0 + jnp.exp(-rows[10]))
    shift_x = rows[0] - centre_x
    shift_y = rows[1] - centre_y
    records = []
    for turn in turns:
        frame = [
            [
                turn[r][0] * local[0][c] + turn[r][1] * local[1][c] + turn[r][2] * local[2][c]
                for c in range(3)
            ]
            for r in range(2)
        ]
        cov_xx = sum(frame[0][c] * frame[0][c] for c in range(3)) + DILATION
        cov_xy = sum(frame[0][c] * frame[1][c] for c in range(3))
        cov_yy = sum(frame[1][c] * frame[1][c] for c in range(3)) + DILATION
        inverse = 1.0 / (cov_xx * cov_yy - cov_xy * cov_xy)
        mean_u = turn[0][0] * shift_x + turn[0][1] * shift_y + turn[0][2] * rows[2] + centre_x
        mean_w = turn[1][0] * shift_x + turn[1][1] * shift_y + turn[1][2] * rows[2] + centre_y
        records.append(
            [mean_u, mean_w, cov_yy * inverse, -cov_xy * inverse, cov_xx * inverse, opacity]
        )
    return records


def blur_taps():
    raw_taps = [math.exp(-(offset - 5) * (offset - 5) / 4.5) for offset in range(11)]
    total = sum(raw_taps)
    return [value / total for value in raw_taps]


NT = (((1,), (1,)), ((), ()))
COLOURS = 3
HALO = 5
MARGIN = 2 * HALO
OUT_LANES = LANES - 2 * MARGIN


def three_parts(value):
    high = value.astype(BF16)
    rest = value - high.astype(F32)
    middle = rest.astype(BF16)
    low = (rest - middle.astype(F32)).astype(BF16)
    return [high, middle, low]


def iota(shape, axis):
    return lax.broadcasted_iota(I32, shape, axis)


def step_kernel(
    sizes,
    params_hbm, visible_hbm, blocks_hbm, counts_hbm, rank_hbm, camera_hbm, backdrop_hbm, target_hbm,
    grad_out, picture_out, loss_out,
    params_v, visible_v, blocks_v, counts_v, rank_v, camera_v, backdrop_v, target_v,
    flat, fields, lists, head, head_space, head_view, out_msg, in_msg, ret_out, ret_in,
    rec, spread, nearer, further, taps_w, inverse, alpha_s, trans_s, seg, spread_in, goal, image,
    rows_buf, goal_buf, cols_buf, adj, moments, view_grads,
    in_sem, head_send, head_recv, camv_send, camv_recv, msg_send, msg_recv, ret_send, ret_recv,
    goal_send, goal_recv, image_send, image_recv, view_send, view_recv,
):
    devices, views, depth, slots, capacity, strip_rows, width_px, splats = sizes
    me = lax.axis_index("space")
    my_view = lax.axis_index("view")
    param_rows = params_v.shape[0]
    tall = splats // LANES
    block_cols = width_px // 16
    block_rows = strip_rows // 8
    groups = -(-width_px // OUT_LANES)
    subs = -(-COLOURS * groups // 8) * 8
    rows_in = strip_rows + 4 * HALO
    rows_mid = strip_rows + 2 * HALO
    centre_x = 0.5 * width_px
    centre_y = 0.5 * strip_rows * devices
    shift = capacity.bit_length() - 1
    taps = blur_taps()
    peers = [lax.rem(me + d, devices) for d in range(1, devices)]
    partners = [lax.rem(my_view + d, views) for d in range(1, views)]

    barrier = pltpu.get_barrier_semaphore()
    goal[...] = jnp.zeros_like(goal)
    image[...] = jnp.zeros_like(image)
    for peer in peers:
        pl.semaphore_signal(barrier, inc=1, device_id={"space": peer}, device_id_type=pl.DeviceIdType.MESH)
    for peer in partners:
        pl.semaphore_signal(barrier, inc=1, device_id={"view": peer}, device_id_type=pl.DeviceIdType.MESH)
    pairs = [
        (blocks_hbm, blocks_v), (counts_hbm, counts_v), (camera_hbm, camera_v), (params_hbm, params_v),
        (visible_hbm.at[0], visible_v), (rank_hbm, rank_v), (backdrop_hbm, backdrop_v), (target_hbm.at[0], target_v),
    ]
    fetches = [pltpu.make_async_copy(a, b, in_sem.at[i]) for i, (a, b) in enumerate(pairs)]
    for fetch in fetches:
        fetch.start()

    lane = iota((1, LANES), 1)
    chunk = lax.shift_right_logical(lane, shift)
    for fetch in fetches[0:3]:
        fetch.wait()
    counted = jnp.zeros((1, LANES), I32)
    for o in range(devices):
        counted = jnp.where(chunk == o, counts_v[:, o : o + 1], counted)
    live = (lane & (capacity - 1)) < counted
    head[...] = jnp.zeros_like(head)
    head[0:1, :] = jnp.where(live, blocks_v[...], -1).astype(F32)
    head[1:2, 0:3] = camera_v[...]
    head_space[me] = head[...]
    head_view[my_view] = head[...]
    pl.semaphore_wait(barrier, devices - 1 + views - 1)
    sends = []

    def remote(src, dst, send, recv, target):
        return pltpu.make_async_remote_copy(
            src_ref=src, dst_ref=dst, send_sem=send, recv_sem=recv, device_id=target,
            device_id_type=pl.DeviceIdType.MESH,
        )

    heads = [remote(head, head_space.at[me], head_send.at[d], head_recv.at[d], {"space": peer}) for d, peer in enumerate(peers)]
    heads += [remote(head, head_view.at[my_view], camv_send.at[d], camv_recv.at[d], {"view": peer}) for d, peer in enumerate(partners)]
    for copy in heads:
        copy.start()

    fetches[3].wait()
    for tile in range(-(-param_rows // 8)):
        size = min(8, param_rows - 8 * tile)
        for i in range(tall):
            start = (tile * tall + i) * 8
            flat[start : start + size, :] = params_v[8 * tile : 8 * tile + size, i * LANES : (i + 1) * LANES]

    def param_row(row):
        return flat[pl.ds(row // 8 * tall * 8 + row % 8, tall, stride=8), :]

    def turn_of(angles):
        return camera_rotation([angles[:, i : i + 1] for i in range(3)])

    turn = turn_of(camera_v[...])
    record = geometry([param_row(i) for i in range(11)], [turn], centre_x, centre_y)[0]
    basis = harmonics(turn[2])
    for c in range(COLOURS):
        colour = 0.5 + basis[0] * param_row(11 + c)
        for i in range(1, 16):
            colour = colour + basis[i] * param_row(11 + 3 * i + c)
        record.append(colour)
    for f in range(9):
        fields[f] = record[f]
    fetches[4].wait()
    listed = jnp.transpose(visible_v[...])
    lists[0] = lax.shift_right_logical(listed, 7)
    lists[1] = listed & (LANES - 1)
    picked = [[] for _ in range(9)]
    for half in range(depth // 8):
        high = lists[0, half * 8 : half * 8 + 8, :]
        low = lists[1, half * 8 : half * 8 + 8, :]
        for f in range(9):
            value = jnp.zeros((8, LANES), F32)
            for h in range(tall):
                row = jnp.broadcast_to(fields[f, h : h + 1, :], (8, LANES))
                row = jnp.take_along_axis(row, low, axis=1, mode="promise_in_bounds")
                value = jnp.where(high == h, row, value)
            picked[f].append(value)
    picked = [jnp.concatenate(p, axis=0) for p in picked]

    per_tile = LANES // capacity

    def pack(values, dst):
        for o in range(devices):
            for t in range(-(-len(values) // per_tile)):
                block = None
                for j, value in enumerate(values[t * per_tile : (t + 1) * per_tile]):
                    moved = pltpu.roll(value, (j - o) * capacity % LANES, axis=1)
                    block = moved if block is None else jnp.where(chunk == j, moved, block)
                dst[o, t * depth : (t + 1) * depth, :] = block

    def unpack(src, f):
        t, j = divmod(f, per_tile)
        value = None
        for s in range(devices):
            moved = pltpu.roll(src[s, t * depth : (t + 1) * depth, :], (s - j) * capacity % LANES, axis=1)
            value = moved if value is None else jnp.where(chunk == s, moved, value)
        return value

    pack(picked, out_msg)
    records_out = [
        remote(out_msg.at[peer], in_msg.at[me], msg_send.at[d], msg_recv.at[d], {"space": peer})
        for d, peer in enumerate(peers)
    ]
    for copy in records_out:
        copy.start()
    in_msg[me] = out_msg[me]

    for copy in heads[0 : devices - 1]:
        copy.wait_recv()
    owned = jnp.zeros((1, LANES), F32)
    for s in range(devices):
        amount = lax.rem(s - me + devices, devices) * capacity
        owned = jnp.where(chunk == s, pltpu.roll(head_space[s], amount, axis=1)[0:1, :], owned)
    owned_i = owned.astype(I32)
    fetches[5].wait()
    ranks = jnp.zeros((1, LANES), I32)
    for s in range(devices):
        ranks = jnp.where(chunk == s, rank_v[:, s : s + 1], ranks)
    square = (LANES, LANES)
    diagonal = iota(square, 0) == iota(square, 1)
    ranks_f = ranks.astype(F32)
    owned_c = jnp.sum(jnp.where(diagonal, owned, 0.0), axis=1, keepdims=True)
    ranks_c = jnp.sum(jnp.where(diagonal, ranks_f, 0.0), axis=1, keepdims=True)
    same = owned_c == owned
    fwd_mask = jnp.where(same & (ranks_c < ranks_f), 1.0, 0.0).astype(BF16)
    bwd_mask = jnp.where(same & (ranks_c > ranks_f), 1.0, 0.0).astype(BF16)
    for part in range(3):
        nearer[part * LANES : (part + 1) * LANES, :] = fwd_mask
        further[part * LANES : (part + 1) * LANES, :] = bwd_mask

    def spread_rows(index, carry):
        band = index // 8
        b = band // groups
        g = band - b * groups
        column = iota((16, LANES), 0) + (OUT_LANES * g - MARGIN + (index - band * 8) * 16)
        place = jnp.where((column >= 0) & (column < width_px), column + b * width_px, -4096)
        for c in range(16):
            spread[pl.ds(pl.multiple_of(index * 16, 16), 16), c * LANES : (c + 1) * LANES] = jnp.where(
                place == owned_i * 16 + c, 1.0, 0.0
            ).astype(BF16)
        return carry

    lax.fori_loop(0, block_rows * groups * 8, spread_rows, 0)

    offset = iota(square, 1) - iota(square, 0)
    taps_high = jnp.zeros(square, F32)
    for i in range(11):
        taps_high = jnp.where(offset == i - HALO, taps[i], taps_high)
    taps_parts = three_parts(taps_high)
    for part in range(3):
        taps_w[part * LANES : (part + 1) * LANES, 0:LANES] = taps_parts[0]
        taps_w[part * LANES : (part + 1) * LANES, LANES : 2 * LANES] = taps_parts[1]

    slot_value = lane.astype(F32)

    def invert(k, total):
        high = lists[0, pl.ds(k, 1), :]
        low = lists[1, pl.ds(k, 1), :]
        hit = iota((tall, LANES), 0) == high
        left = jnp.concatenate(
            [jnp.where(hit, slot_value, 0.0), jnp.where(hit, k.astype(F32), 0.0)], axis=0
        ).astype(BF16)
        right = jnp.where(iota(square, 0) == low, 1.0, 0.0).astype(BF16)
        return total + lax.dot_general(left, right, NT, preferred_element_type=F32)

    inverse[...] = lax.fori_loop(0, depth, invert, jnp.zeros((2 * tall, LANES), F32)).astype(I32)

    def column_of(g):
        return lane + (OUT_LANES * g - MARGIN)

    def to_groups(natural, g):
        first = OUT_LANES * g - MARGIN
        left, by = divmod(first, LANES)
        value = jnp.zeros((8, LANES), F32)
        for piece in (left, left + 1):
            if 0 <= piece < width_px // LANES:
                moved = pltpu.roll(natural[:, piece * LANES : (piece + 1) * LANES], -by % LANES, axis=1)
                keep = (lane < LANES - by) if piece == left else (lane >= LANES - by)
                value = jnp.where(keep, moved, value)
        return value

    def own_rows(b, sub):
        return pl.ds((MARGIN + b * 8) * subs + sub, 8, stride=subs)

    fetches[7].wait()
    for ch in range(COLOURS):
        for b in range(block_rows):
            natural = target_v[ch, b * 8 : b * 8 + 8, :]
            for g in range(groups):
                goal[own_rows(b, ch * groups + g), :] = to_groups(natural, g)

    reach = MARGIN * subs
    top, bottom = MARGIN * subs, strip_rows * subs

    def exchange(ref, send, recv):
        upward = remote(
            ref.at[pl.ds(top, reach)], ref.at[pl.ds((MARGIN + strip_rows) * subs, reach)],
            send.at[0], recv.at[0], {"space": lax.rem(me + devices - 1, devices)},
        )
        downward = remote(
            ref.at[pl.ds(bottom, reach)], ref.at[pl.ds(0, reach)],
            send.at[1], recv.at[1], {"space": lax.rem(me + 1, devices)},
        )
        return upward, downward

    not_first, not_last = me > 0, me < devices - 1

    def begin(copies):
        pl.when(not_first)(copies[0].start)
        pl.when(not_last)(copies[1].start)

    def arrived(copies):
        pl.when(not_last)(copies[0].wait_recv)
        pl.when(not_first)(copies[1].wait_recv)

    def left(copies):
        pl.when(not_first)(copies[0].wait_send)
        pl.when(not_last)(copies[1].wait_send)

    goal_copies = exchange(goal, goal_send, goal_recv)
    begin(goal_copies)

    for copy in records_out:
        copy.wait_recv()
    own_ids = jnp.maximum(owned, 0.0)
    block_y = jnp.floor((own_ids + 0.5) * (1.0 / block_cols))
    block_x = own_ids - block_y * block_cols
    corner_x = block_x * 16.0 + 0.5
    corner_y = block_y * 8.0 + (me * strip_rows).astype(F32) + 0.5
    got = [unpack(in_msg, f) for f in range(9)]
    rec[0] = corner_x - got[0]
    rec[1] = corner_y - got[1]
    rec[2] = -0.5 * LOG2E * got[2]
    rec[3] = -LOG2E * got[3]
    rec[4] = -0.5 * LOG2E * got[4]
    rec[5] = jnp.log2(got[5])
    for f in range(6, 9):
        rec[f] = got[f]
    for f in range(2, 6):
        rec[7 + f] = got[f]
    vreg = (8, LANES)
    rows_f = iota(vreg, 0).astype(F32)

    def wide(f, k):
        return jnp.broadcast_to(rec[f, k : k + 1, :], vreg)

    width_c = 4

    def render_some(index, carry):
        trans = [jnp.ones(vreg, F32)] * width_c
        logs = [jnp.zeros(vreg, F32)] * width_c
        run = [None] * width_c
        sums = [[jnp.zeros(vreg, F32)] * width_c for _ in range(COLOURS)]
        base = (index * width_c).astype(F32)
        for k in range(depth):
            delta_y = wide(1, k) + rows_f
            cross = wide(3, k) * delta_y
            square_y = wide(4, k) * delta_y * delta_y + wide(5, k)
            first_x = wide(0, k) + base
            curve = wide(2, k)
            tint = [wide(6 + ch, k) for ch in range(COLOURS)]
            for j in range(width_c):
                delta_x = first_x + float(j)
                alpha = jnp.exp2((curve * delta_x + cross) * delta_x + square_y)
                place = pl.ds(pl.multiple_of((index * width_c + j) * 8, 8), 8)
                alpha_s[k, place, :] = alpha
                trans_s[k, place, :] = trans[j]
                weight = alpha * trans[j]
                for ch in range(COLOURS):
                    sums[ch][j] = sums[ch][j] + weight * tint[ch]
                kept = 1.0 - alpha
                trans[j] = trans[j] * kept
                run[j] = kept if k % 4 == 0 else run[j] * kept
                if k % 4 == 3 or k == depth - 1:
                    logs[j] = logs[j] + jnp.log(run[j])
        for j in range(width_c):
            place = pl.ds(pl.multiple_of((index * width_c + j) * 8, 8), 8)
            for ch in range(COLOURS):
                seg[ch, place, :] = sums[ch][j]
            seg[3, place, :] = trans[j]
            seg[4, place, :] = logs[j]
        return carry

    lax.fori_loop(0, 16 // width_c, render_some, 0)

    before = jnp.dot(
        jnp.concatenate(three_parts(seg[4]), axis=1), nearer[...], preferred_element_type=F32
    )
    seg[4] = jnp.exp(before)
    fetches[6].wait()
    backs = [backdrop_v[:, ch : ch + 1] for ch in range(COLOURS)]
    spread_in[COLOURS * 8 : COLOURS * 8 + 8, :] = jnp.zeros((8, 16 * LANES), F32)
    for c in range(16):
        part = slice(c * 8, c * 8 + 8)
        share = seg[4, part, :]
        taken = 1.0 - seg[3, part, :]
        for ch in range(COLOURS):
            tinted = seg[ch, part, :] - backs[ch] * taken
            seg[ch, part, :] = tinted
            spread_in[ch * 8 : ch * 8 + 8, c * LANES : (c + 1) * LANES] = share * tinted
    rows32 = COLOURS * 8 + 8
    spread_out = lax.dot_general(
        jnp.concatenate(three_parts(spread_in[...]), axis=0), spread[...], NT, preferred_element_type=F32
    )
    spread_out = spread_out[0:rows32] + spread_out[rows32 : 2 * rows32] + spread_out[2 * rows32 : 3 * rows32]
    for g in range(groups):
        on_image = (column_of(g) >= 0) & (column_of(g) < width_px)
        for ch in range(COLOURS):
            for b in range(block_rows):
                value = spread_out[ch * 8 : ch * 8 + 8, (b * groups + g) * LANES : (b * groups + g + 1) * LANES]
                image[own_rows(b, ch * groups + g), :] = value + jnp.where(on_image, backs[ch], 0.0)
    image_copies = exchange(image, image_send, image_recv)
    begin(image_copies)

    for ch in range(COLOURS):
        for b in range(block_rows):
            for j in range(width_px // LANES):
                natural = jnp.zeros(vreg, F32)
                for g in range(groups):
                    first = OUT_LANES * g
                    if first < (j + 1) * LANES and first + OUT_LANES > j * LANES:
                        moved = pltpu.roll(
                            image[own_rows(b, ch * groups + g), :], (first - MARGIN - j * LANES) % LANES, axis=1
                        )
                        here = lane + j * LANES
                        natural = jnp.where((here >= first) & (here < first + OUT_LANES), moved, natural)
                picture_out[0, ch, b * 8 : b * 8 + 8, j * LANES : (j + 1) * LANES] = natural

    def blur_rows(load, count, store):
        for half in range(subs // 8):
            lines = [load(y, half) for y in range(count + 10)]
            for y in range(count):
                total = taps[5] * lines[y + 5]
                for i in range(5):
                    total = total + taps[i] * (lines[y + i] + lines[y + 10 - i])
                store(y, half, total)

    def reader(ref):
        return lambda y, half: ref[y * subs + half * 8 : y * subs + half * 8 + 8, :]

    def writer(ref, base):
        def store(y, half, value):
            ref[base + y * subs + half * 8 : base + y * subs + half * 8 + 8, :] = value

        return store

    def blur_columns(value):
        both = jnp.dot(jnp.concatenate(three_parts(value), axis=1), taps_w[...], preferred_element_type=F32)
        return both[:, 0:LANES] + both[:, LANES : 2 * LANES]

    mid = rows_mid * subs
    from_goal, from_image = reader(goal), reader(image)
    arrived(goal_copies)
    blur_rows(from_goal, rows_mid, writer(rows_buf, 0))
    blur_rows(lambda y, h: from_goal(y, h) * from_goal(y, h), rows_mid, writer(rows_buf, mid))
    goal_buf[...] = blur_columns(rows_buf[0 : 2 * mid, :])

    arrived(image_copies)
    blur_rows(from_image, rows_mid, writer(rows_buf, 0))
    blur_rows(lambda y, h: from_image(y, h) * from_image(y, h), rows_mid, writer(rows_buf, mid))
    blur_rows(lambda y, h: from_image(y, h) * from_goal(y, h), rows_mid, writer(rows_buf, 2 * mid))
    cols_buf[...] = blur_columns(rows_buf[...])

    two = 2 * subs
    sub_row = iota((two, LANES), 0)
    upper = sub_row >= subs
    in_sub = jnp.where(upper, sub_row - subs, sub_row)
    for _ in range(COLOURS - 1):
        in_sub = jnp.where(in_sub >= groups, in_sub - groups, in_sub)
    own_column = iota((two, LANES), 1) + in_sub * OUT_LANES - MARGIN
    used = jnp.where(upper, sub_row - subs, sub_row) < COLOURS * groups
    on_columns = (own_column >= 0) & (own_column < width_px) & used
    inner = (iota((two, LANES), 1) >= MARGIN) & (iota((two, LANES), 1) < MARGIN + OUT_LANES)
    height_px = strip_rows * devices

    def similarity(index, total):
        at = pl.multiple_of(index * two, 8)
        mean_a = cols_buf[pl.ds(at, two), :]
        raw_aa = cols_buf[pl.ds(at + mid, two), :]
        raw_ab = cols_buf[pl.ds(at + 2 * mid, two), :]
        mean_b = goal_buf[pl.ds(at, two), :]
        raw_bb = goal_buf[pl.ds(at + mid, two), :]
        pixel_a = image[pl.ds(at + HALO * subs, two), :]
        pixel_b = goal[pl.ds(at + HALO * subs, two), :]
        line = index * 2 + jnp.where(upper, 1, 0)
        y = line + (me * strip_rows - HALO)
        counted_here = on_columns & (y >= 0) & (y < height_px)
        square_a, square_b, cross = mean_a * mean_a, mean_b * mean_b, mean_a * mean_b
        first_n = 2.0 * cross + SSIM_FIRST
        second_n = 2.0 * (raw_ab - cross) + SSIM_SECOND
        first_d = square_a + square_b + SSIM_FIRST
        second_d = (raw_aa - square_a) + (raw_bb - square_b) + SSIM_SECOND
        scale = 1.0 / (first_d * second_d)
        ssim = first_n * second_n * scale
        inv_first, inv_second = second_d * scale, first_d * scale
        seed = jnp.where(counted_here, -0.2, 0.0)
        by_aa = -ssim * inv_second
        by_ab = 2.0 * first_n * scale
        by_a = 2.0 * (mean_b * second_n * scale - mean_a * (ssim * inv_first + by_aa)) - mean_b * by_ab
        adj[pl.ds(at, two), :] = seed * by_a
        adj[pl.ds(at + mid, two), :] = seed * by_aa
        adj[pl.ds(at + 2 * mid, two), :] = seed * by_ab
        differ = pixel_a - pixel_b
        term = 0.8 * jnp.sqrt(differ * differ + SMOOTHING) + 0.2 * (1.0 - ssim)
        own = counted_here & inner & (line >= HALO) & (line < HALO + strip_rows)
        return total + jnp.where(own, term, 0.0)

    own_terms = lax.fori_loop(0, rows_mid // 2, similarity, jnp.zeros((two, LANES), F32))
    own_loss = jnp.sum(jnp.sum(own_terms, axis=1, keepdims=True), axis=0, keepdims=True)

    end = strip_rows * subs
    for q in range(3):
        blur_rows(lambda y, h: reader(adj)(y + q * rows_mid, h), strip_rows, writer(rows_buf, q * end))
    cols_buf[0 : 3 * end, :] = blur_columns(rows_buf[0 : 3 * end, :])

    def pixel_grad(index, carry):
        at = pl.multiple_of(index * two, 8)
        pixel_a = image[pl.ds(at + MARGIN * subs, two), :]
        pixel_b = goal[pl.ds(at + MARGIN * subs, two), :]
        differ = pixel_a - pixel_b
        value = (
            cols_buf[pl.ds(at, two), :]
            + 2.0 * pixel_a * cols_buf[pl.ds(at + end, two), :]
            + pixel_b * cols_buf[pl.ds(at + 2 * end, two), :]
            + 0.8 * differ / jnp.sqrt(differ * differ + SMOOTHING)
        )
        adj[pl.ds(at, two), :] = jnp.where(on_columns & inner, value, 0.0)
        return carry

    lax.fori_loop(0, strip_rows // 2, pixel_grad, 0)

    pulled = []
    for ch in range(COLOURS):
        pulled.append(
            jnp.concatenate(
                [
                    adj[pl.ds(b * 8 * subs + ch * groups + g, 8, stride=subs), :]
                    for b in range(block_rows)
                    for g in range(groups)
                ],
                axis=1,
            )
        )
    pulled.append(jnp.zeros_like(pulled[0]))
    pulled = jnp.dot(
        jnp.concatenate(three_parts(jnp.concatenate(pulled, axis=0)), axis=0),
        spread[...],
        preferred_element_type=F32,
    )
    spread_in[...] = pulled[0:rows32] + pulled[rows32 : 2 * rows32] + pulled[2 * rows32 : 3 * rows32]
    for c in range(16):
        part = slice(c * 8, c * 8 + 8)
        share = seg[4, part, :]
        by_share, by_trans = None, None
        for ch in range(COLOURS):
            grad = spread_in[ch * 8 : ch * 8 + 8, c * LANES : (c + 1) * LANES]
            piece = grad * seg[ch, part, :]
            by_share = piece if by_share is None else by_share + piece
            grad = grad * share
            seg[ch, part, :] = grad
            piece = grad * backs[ch]
            by_trans = piece if by_trans is None else by_trans + piece
        rows_buf[part, :] = by_share * share
        cols_buf[part, :] = by_trans
    by_log = jnp.dot(
        jnp.concatenate(three_parts(rows_buf[0:LANES, :]), axis=1), further[...], preferred_element_type=F32
    )
    trans = seg[3]
    visible_through = trans > 2e-38
    cols_buf[0:LANES, :] += jnp.where(visible_through, by_log / jnp.where(visible_through, trans, 1.0), 0.0)

    def unrender(step, carry):
        k = depth - 1 - step
        row = pl.ds(k, 1)

        def across(f):
            return jnp.broadcast_to(rec[f, row, :], vreg)

        delta_y = across(1) + rows_f
        first_x = across(0)
        tint = [across(6 + ch) for ch in range(COLOURS)]
        sums = [jnp.zeros(vreg, F32)] * 6
        for c in range(16):
            part = slice(c * 8, c * 8 + 8)
            alpha = alpha_s[k, part, :]
            weight = alpha * trans_s[k, part, :]
            behind = cols_buf[part, :]
            grads = [seg[ch, part, :] for ch in range(COLOURS)]
            gap = grads[0] * tint[0] + grads[1] * tint[1] + grads[2] * tint[2] - behind
            cols_buf[part, :] = behind + alpha * gap
            slope = weight * gap
            delta_x = first_x + float(c)
            slope_x = slope * delta_x
            terms = [slope, slope_x, slope_x * delta_x] + [weight * g for g in grads]
            sums = [a + b for a, b in zip(sums, terms)]
        rows = [
            sums[0], sums[1], sums[0] * delta_y, sums[2], sums[1] * delta_y, sums[0] * delta_y * delta_y,
            sums[3], sums[4], sums[5],
        ]
        for f, value in enumerate(rows):
            moments[f, row, :] = jnp.sum(value, axis=0, keepdims=True)
        return carry

    lax.fori_loop(0, depth, unrender, 0)
    conic_a, conic_b, conic_c, opaque = [rec[9 + i] for i in range(4)]
    grads_out = [
        conic_a * moments[1] + conic_b * moments[2],
        conic_b * moments[1] + conic_c * moments[2],
        -0.5 * moments[3],
        -moments[4],
        -0.5 * moments[5],
        moments[0] / opaque,
        moments[6],
        moments[7],
        moments[8],
        jnp.broadcast_to(own_loss, (depth, LANES)),
    ]
    pack(grads_out, ret_out)
    grads_back = [
        remote(ret_out.at[peer], ret_in.at[me], ret_send.at[d], ret_recv.at[d], {"space": peer})
        for d, peer in enumerate(peers)
    ]
    for copy in grads_back:
        copy.start()
    ret_in[me] = ret_out[me]
    for copy in grads_back:
        copy.wait_recv()

    for f in range(9):
        fields[f] = unpack(ret_in, f)
    tile, j = divmod(9, per_tile)
    total_loss = jnp.zeros((1, 1), F32)
    for s in range(devices):
        total_loss = total_loss + ret_in[s, tile * depth : tile * depth + 1, j * capacity : j * capacity + 1]
    loss_out[...] = total_loss / (3.0 * height_px * width_px)
    for half in range(tall // 8):
        slot_of = inverse[half * 8 : half * 8 + 8, :]
        entry_of = inverse[tall + half * 8 : tall + half * 8 + 8, :]
        for f in range(9):
            value = jnp.zeros(vreg, F32)
            for h in range(depth):
                row = jnp.broadcast_to(fields[f, h : h + 1, :], vreg)
                row = jnp.take_along_axis(row, slot_of, axis=1, mode="promise_in_bounds")
                value = jnp.where(entry_of == h, row, value)
            view_grads[my_view, f, half * 8 : half * 8 + 8, :] = value
    views_out = [
        remote(view_grads.at[my_view], view_grads.at[my_view], view_send.at[d], view_recv.at[d], {"view": peer})
        for d, peer in enumerate(partners)
    ]
    for copy in views_out:
        copy.start()
    for copy in heads[devices - 1 :]:
        copy.wait_recv()
    turns = [turn_of(head_view[v, 1:2, :]) for v in range(views)]
    bases = [harmonics(turn[2]) for turn in turns]
    for copy in views_out:
        copy.wait_recv()

    def put_row(row, value):
        flat[pl.ds(row // 8 * tall * 8 + row % 8, tall, stride=8), :] = value

    pull = jax.vjp(lambda r: geometry(r, turns, centre_x, centre_y), [param_row(i) for i in range(11)])[1]
    for i, value in enumerate(pull([[view_grads[v, f] for f in range(6)] for v in range(views)])[0]):
        put_row(i, value)
    for c in range(COLOURS):
        by_colour = [view_grads[v, 6 + c] for v in range(views)]
        for i in range(16):
            value = bases[0][i] * by_colour[0]
            for v in range(1, views):
                value = value + bases[v][i] * by_colour[v]
            put_row(11 + 3 * i + c, value)
    for tile in range(-(-param_rows // 8)):
        size = min(8, param_rows - 8 * tile)
        for i in range(tall):
            start = (tile * tall + i) * 8
            grad_out[8 * tile : 8 * tile + size, i * LANES : (i + 1) * LANES] = flat[start : start + size, :]
    for copy in heads + records_out + grads_back + views_out:
        copy.wait_send()
    left(goal_copies)
    left(image_copies)


def shards(params, visible, blocks, counts, depth_rank, camera, background, target):
    devices, views = lax.axis_size("space"), lax.axis_size("view")
    slots, depth = visible.shape[1:]
    capacity = slots // devices
    strip_rows, width_px = target.shape[2:]
    splats = params.shape[1]
    tall = splats // LANES
    groups = -(-width_px // OUT_LANES)
    subs = -(-COLOURS * groups // 8) * 8
    rows_in, rows_mid = strip_rows + 4 * HALO, strip_rows + 2 * HALO
    sizes = (devices, views, depth, slots, capacity, strip_rows, width_px, splats)
    per_tile = LANES // capacity
    tiles_out, tiles_back = -(-9 // per_tile), -(-10 // per_tile)
    vmem = lambda *shape: pltpu.VMEM(shape, F32)
    dma = lambda count: pltpu.SemaphoreType.DMA((count,))
    scratch = [
        vmem(*params.shape), pltpu.VMEM((slots, depth), I32), pltpu.VMEM(blocks.shape, I32),
        pltpu.VMEM(counts.shape, I32), pltpu.VMEM(depth_rank.shape, I32), vmem(*camera.shape),
        vmem(*background.shape), vmem(*target.shape[1:]),
        vmem(-(-params.shape[0] // 8) * tall * 8, LANES), vmem(9, tall, LANES), pltpu.VMEM((2, depth, LANES), I32),
        vmem(8, LANES), vmem(devices, 8, LANES), vmem(views, 8, LANES),
        vmem(devices, tiles_out * depth, LANES), vmem(devices, tiles_out * depth, LANES),
        vmem(devices, tiles_back * depth, LANES), vmem(devices, tiles_back * depth, LANES),
        vmem(13, depth, LANES), pltpu.VMEM((strip_rows // 8 * groups * LANES, 16 * LANES), BF16),
        pltpu.VMEM((3 * LANES, LANES), BF16), pltpu.VMEM((3 * LANES, LANES), BF16),
        pltpu.VMEM((3 * LANES, 2 * LANES), BF16), pltpu.VMEM((2 * tall, LANES), I32),
        vmem(depth, LANES, LANES), vmem(depth, LANES, LANES), vmem(5, LANES, LANES),
        vmem(COLOURS * 8 + 8, 16 * LANES), vmem(rows_in * subs, LANES), vmem(rows_in * subs, LANES),
        vmem(3 * rows_mid * subs, LANES), vmem(2 * rows_mid * subs, LANES), vmem(3 * rows_mid * subs, LANES),
        vmem(3 * rows_mid * subs, LANES), vmem(9, depth, LANES), vmem(views, 9, tall, LANES),
        dma(8), dma(devices), dma(devices), dma(views), dma(views), dma(devices), dma(devices), dma(devices),
        dma(devices), dma(2), dma(2), dma(2), dma(2), dma(views), dma(views),
    ]
    grad, picture, loss = pl.pallas_call(
        functools.partial(step_kernel, sizes),
        name="step",
        out_shape=(
            jax.ShapeDtypeStruct(params.shape, F32),
            jax.ShapeDtypeStruct(target.shape, F32),
            jax.ShapeDtypeStruct((1, 1), F32),
        ),
        in_specs=[pl.BlockSpec(memory_space=pl.ANY)] * 8,
        out_specs=tuple([pl.BlockSpec(memory_space=pltpu.VMEM)] * 3),
        scratch_shapes=scratch,
        compiler_params=pltpu.CompilerParams(collective_id=0, has_side_effects=True),
    )(params, visible, blocks, counts, depth_rank, camera, background, target)
    return (grad, picture, loss.reshape(1))


def solution(mesh):
    in_specs = (
        P(None, "space"),
        P("space", None, None),
        P("space", None),
        P("space", None),
        P("view", None),
        P("view", None),
        P("view", None),
        P("view", None, "space", None),
    )
    out_specs = (P(None, "space"), P("view", None, "space", None), P("view"))
    return jax.shard_map(shards, mesh=mesh, in_specs=in_specs, out_specs=out_specs, check_vma=False)
```

time: 115 us -> 45.7 us (0.40)
  Pallas kernels: 12.8 us -> 38.9 us
  other arithmetic: 23.9 us -> 0 us
  waiting for transfers between devices: 19.7 us -> 0 us
  starting transfers between devices: 15.6 us -> 0 us
  matrix products: 14.2 us -> 0 us
  local copies, waits for them, and re-layouts: 16.5 us -> 3.98 us
  blocking collectives: 8.15 us -> 0 us
    pallas_call x3 -> x1, Pallas kernels: 12.8 us -> 38.9 us  [shards(): pl.pallas_call(functools.partial(step_kernel, sizes), name='step', out_sh...]
    dot_general x7 -> x0, matrix products: 14.2 us -> none  [the longest x3 12 us: render(): jnp.einsum('skp,csk->scp', weights, gathered[6:9], precision=HIGHEST)]
    all_to_all x2 -> x0, waiting for transfers between devices: 13.6 us -> none  [the longest x1 7.32 us: shards(): lax.all_to_all(message, 'space', split_axis=0, concat_axis=0, tiled=True)]
    all_to_all x2 -> x0, starting transfers between devices: 12 us -> none  [the longest x1 7.31 us: shards(): lax.all_to_all(message, 'space', split_axis=0, concat_axis=0, tiled=True)]
    all_gather x1 -> x0, blocking collectives: 8.15 us -> none  [shards(): every_view = lax.all_gather(grad_records, 'view', axis=0, tiled=False)]
    reduce_sum x5 -> x0, other arithmetic: 7.03 us -> none  [the longest x1 5.58 us: render(): gathered[4][:, :, None] * delta_y * delta_y]
    ppermute x2 -> x0, waiting for transfers between devices: 6.06 us -> none  [the longest x1 5.9 us: with_halo(): before = lax.ppermute(last, axis, up)]
    mul x16 -> x0, other arithmetic: 4.59 us -> none  [the longest x1 1.44 us: pixel_terms(): (2.0 * mean_a * mean_b + SSIM_FIRST) * (2.0 * cov_ab + SSIM_SECOND)]
  transfers between devices with their start and end apart: 4 -> 0, of which waited for: 4 -> 0; matrix products, arithmetic and copies ran while one was open for 1% -> 0% of each run, Pallas kernels for 0% -> 0%
where the time goes in v1:
time: 45.7 us; the launch traced here: 45.3 us
  Pallas kernels  38.9 us (85%)
  local copies, waits for them, and re-layouts  3.98 us (9%)
  between operations  2.4 us (5%)
    pallas_call x1, Pallas kernels, shards(): pl.pallas_call(functools.partial(step_kernel, sizes), name='step', out_sh...  38.9 us
    unnamed x5, local copies, waits for them, and re-layouts  3.98 us

profile of v1, /device:TPU:0, one launch (start us, length us, event | category | flops | bytes accessed | tf_op | source)
XLA Modules:
  0.0 45.3 jit_solution(6206450754777117558)
XLA Ops:
  0.6 1.4 %copy.11.visible_hbm = s32[1,128,16]{2,1,0:T(8,128)} copy(s32[1,128,16]{1,2,0:T(8,128)} %param.9) | data formatting | bytes 16384 | tf_op args[1]
  2.1 38.9 %step.1 = (f32[59,2048]{1,0:T(8,128)}, f32[1,3,16,512]{3,2,1,0:T(8,128)}, f32[1,1]{1,0:T(1,128)}) custom-call(f32[59,2048]{1,0:T(8,128)} %params_hbm.1, s32[1,128,16]{2,1,0:T(8,128)} %copy.11.visible_hbm, s32[1,128]{1,0:T(1,128)} %blocks_hbm.1, s32[1,8]{1,0:T(1,128)} %counts_hbm.1, s32[1,8]{1,0:T(1,128)} %rank_hbm.1, f32[1,3]{1,0:T(1,128)} %camera_hbm.1, ...), custom_call_target="tpu_custom_call" | custom-call | tf_op jit(solution)/shard_map/step/pallas_call | solution.py:793
  41.0 0.0 copy-start
  41.0 1.9 %copy.15 = f32[59,2048]{1,0:T(8,128)} copy(f32[59,2048]{1,0:T(8,128)} %get-tuple-element.12) | data formatting | bytes 966656
  42.9 0.0 copy-done
  42.9 0.6 %copy.16 = f32[1,3,16,512]{3,2,1,0:T(8,128)} copy(f32[1,3,16,512]{3,2,1,0:T(8,128)S(1)} %copy-done) | data formatting | bytes 196608
Async XLA Ops:
  41.0 1.9 %copy-start = (f32[1,3,16,512]{3,2,1,0:T(8,128)S(1)}, f32[1,3,16,512]{3,2,1,0:T(8,128)}, u32[]{:S(2)}) copy-start(f32[1,3,16,512]{3,2,1,0:T(8,128)} %get-tuple-element.13) | copy-start | bytes 294916

commit v2 on v1

v2 whole, which is shorter than its diff:
```python
import functools
import math

import jax
import jax.numpy as jnp
import numpy as np
from jax import lax
from jax.experimental import pallas as pl
from jax.experimental.pallas import tpu as pltpu
from jax.sharding import PartitionSpec as P

F32 = jnp.float32
BF16 = jnp.bfloat16
I32 = jnp.int32
LANES = 128
LOG2E = 1.4426950408889634
SH_ZERO = 0.28209479177387814
SH_ONE = 0.4886025119029199
SH_TWO = (
    1.0925484305920792,
    -1.0925484305920792,
    0.31539156525252005,
    -1.0925484305920792,
    0.5462742152960396,
)
SH_THREE = (
    -0.5900435899266435,
    2.890611442640554,
    -0.4570457994644658,
    0.3731763325901154,
    -0.4570457994644658,
    1.445305721320277,
    -0.5900435899266435,
)
DILATION = 0.3
SMOOTHING = 0.0001
SSIM_FIRST = 0.0001
SSIM_SECOND = 0.0009


def camera_rotation(angles):
    cos_a, sin_a = (jnp.cos(angles[0]), jnp.sin(angles[0]))
    cos_b, sin_b = (jnp.cos(angles[1]), jnp.sin(angles[1]))
    cos_c, sin_c = (jnp.cos(angles[2]), jnp.sin(angles[2]))
    return [
        [cos_c * cos_b, cos_c * sin_b * sin_a - sin_c * cos_a, cos_c * sin_b * cos_a + sin_c * sin_a],
        [sin_c * cos_b, sin_c * sin_b * sin_a + cos_c * cos_a, sin_c * sin_b * cos_a - cos_c * sin_a],
        [-sin_b, cos_b * sin_a, cos_b * cos_a],
    ]


def harmonics(view_axis):
    axis_x, axis_y, axis_z = (view_axis[0], view_axis[1], view_axis[2])
    sq_x, sq_y, sq_z = (axis_x * axis_x, axis_y * axis_y, axis_z * axis_z)
    return [
        SH_ZERO * jnp.ones_like(axis_x),
        -SH_ONE * axis_y,
        SH_ONE * axis_z,
        -SH_ONE * axis_x,
        SH_TWO[0] * axis_x * axis_y,
        SH_TWO[1] * axis_y * axis_z,
        SH_TWO[2] * (2.0 * sq_z - sq_x - sq_y),
        SH_TWO[3] * axis_x * axis_z,
        SH_TWO[4] * (sq_x - sq_y),
        SH_THREE[0] * axis_y * (3.0 * sq_x - sq_y),
        SH_THREE[1] * axis_x * axis_y * axis_z,
        SH_THREE[2] * axis_y * (4.0 * sq_z - sq_x - sq_y),
        SH_THREE[3] * axis_z * (2.0 * sq_z - 3.0 * sq_x - 3.0 * sq_y),
        SH_THREE[4] * axis_x * (4.0 * sq_z - sq_x - sq_y),
        SH_THREE[5] * axis_z * (sq_x - sq_y),
        SH_THREE[6] * axis_x * (sq_x - 3.0 * sq_y),
    ]


def geometry(rows, turns, centre_x, centre_y):
    scales = [jnp.exp(rows[i]) for i in range(3, 6)]
    quat = rows[6:10]
    length = jnp.sqrt(quat[0] * quat[0] + quat[1] * quat[1] + quat[2] * quat[2] + quat[3] * quat[3])
    part_w, part_x, part_y, part_z = [q / length for q in quat]
    spin = [
        [
            1.0 - 2.0 * (part_y * part_y + part_z * part_z),
            2.0 * (part_x * part_y - part_w * part_z),
            2.0 * (part_x * part_z + part_w * part_y),
        ],
        [
            2.0 * (part_x * part_y + part_w * part_z),
            1.0 - 2.0 * (part_x * part_x + part_z * part_z),
            2.0 * (part_y * part_z - part_w * part_x),
        ],
        [
            2.0 * (part_x * part_z - part_w * part_y),
            2.0 * (part_y * part_z + part_w * part_x),
            1.0 - 2.0 * (part_x * part_x + part_y * part_y),
        ],
    ]
    local = [[spin[r][c] * scales[c] for c in range(3)] for r in range(3)]
    opacity = 1.0 / (1.0 + jnp.exp(-rows[10]))
    shift_x = rows[0] - centre_x
    shift_y = rows[1] - centre_y
    records = []
    for turn in turns:
        frame = [
            [
                turn[r][0] * local[0][c] + turn[r][1] * local[1][c] + turn[r][2] * local[2][c]
                for c in range(3)
            ]
            for r in range(2)
        ]
        cov_xx = sum(frame[0][c] * frame[0][c] for c in range(3)) + DILATION
        cov_xy = sum(frame[0][c] * frame[1][c] for c in range(3))
        cov_yy = sum(frame[1][c] * frame[1][c] for c in range(3)) + DILATION
        inverse = 1.0 / (cov_xx * cov_yy - cov_xy * cov_xy)
        mean_u = turn[0][0] * shift_x + turn[0][1] * shift_y + turn[0][2] * rows[2] + centre_x
        mean_w = turn[1][0] * shift_x + turn[1][1] * shift_y + turn[1][2] * rows[2] + centre_y
        records.append(
            [mean_u, mean_w, cov_yy * inverse, -cov_xy * inverse, cov_xx * inverse, opacity]
        )
    return records


def blur_taps():
    raw_taps = [math.exp(-(offset - 5) * (offset - 5) / 4.5) for offset in range(11)]
    total = sum(raw_taps)
    return [value / total for value in raw_taps]


NT = (((1,), (1,)), ((), ()))
COLOURS = 3
HALO = 5
MARGIN = 2 * HALO
TABLE = 32


def three_parts(value):
    high = value.astype(BF16)
    rest = value - high.astype(F32)
    middle = rest.astype(BF16)
    low = (rest - middle.astype(F32)).astype(BF16)
    return [high, middle, low]


def iota(shape, axis):
    return lax.broadcasted_iota(I32, shape, axis)


def swap_chunks(values, width):
    lane = iota((1, LANES), 1)
    for bit in range(3):
        step = 1 << bit
        low = (lane & (width * step)) == 0
        moved = list(values)
        for a in range(8):
            if not a & step:
                first, second = values[a], values[a | step]
                moved[a] = jnp.where(low, first, pltpu.roll(second, width * step, axis=1))
                moved[a | step] = jnp.where(low, pltpu.roll(first, LANES - width * step, axis=1), second)
        values = moved
    return values


def swap_sublanes(value, width):
    lane, row = iota((8, LANES), 1), iota((8, LANES), 0)
    for bit in range(3):
        step = 1 << bit
        low_lane, low_row = (lane & (width * step)) == 0, (row & step) == 0
        up = pltpu.roll(pltpu.roll(value, 8 - step, axis=0), width * step, axis=1)
        down = pltpu.roll(pltpu.roll(value, step, axis=0), LANES - width * step, axis=1)
        value = jnp.where(low_lane == low_row, value, jnp.where(low_row, up, down))
    return value


def step_kernel(
    sizes,
    params_hbm, visible_hbm, blocks_hbm, counts_hbm, rank_hbm, camera_hbm, backdrop_hbm, target_hbm,
    view_grads, table_out, picture_out, loss_out,
    params_v, visible_v, blocks_v, counts_v, rank_v, camera_v, backdrop_v, target_v,
    flat, fields, lists, head, head_view, out_msg, in_msg, ret_out, ret_in,
    rec, place_f, place_b, nearer, further, taps_w, inverse, alpha_s, trans_s, seg, goal, image,
    rows_buf, goal_buf, cols_buf, adj, seed_s, own_s, moments,
    in_sem, camv_send, camv_recv, msg_send, msg_recv, ret_send, ret_recv,
    goal_send, goal_recv, image_send, image_recv, view_send, view_recv,
):
    devices, views, depth, slots, capacity, strip_rows, width_px, splats = sizes
    me = lax.axis_index("space")
    my_view = lax.axis_index("view")
    param_rows = params_v.shape[0]
    tall = splats // LANES
    block_cols = width_px // 16
    block_rows = strip_rows // 8
    groups = width_px // LANES
    subs = COLOURS * groups
    bands = block_rows * groups
    rows_in = strip_rows + 4 * HALO
    rows_mid = strip_rows + 2 * HALO
    centre_x = 0.5 * width_px
    centre_y = 0.5 * strip_rows * devices
    shift = capacity.bit_length() - 1
    taps = blur_taps()
    peers = [lax.rem(me + d, devices) for d in range(1, devices)]
    partners = [lax.rem(my_view + d, views) for d in range(1, views)]

    barrier = pltpu.get_barrier_semaphore()
    goal[...] = jnp.zeros_like(goal)
    image[...] = jnp.zeros_like(image)
    for peer in peers:
        pl.semaphore_signal(barrier, inc=1, device_id={"space": peer}, device_id_type=pl.DeviceIdType.MESH)
    for peer in partners:
        pl.semaphore_signal(barrier, inc=1, device_id={"view": peer}, device_id_type=pl.DeviceIdType.MESH)
    pairs = [
        (blocks_hbm, blocks_v), (counts_hbm, counts_v), (camera_hbm, camera_v), (params_hbm, params_v),
        (visible_hbm.at[0], visible_v), (rank_hbm, rank_v), (backdrop_hbm, backdrop_v), (target_hbm.at[0], target_v),
    ]
    fetches = [pltpu.make_async_copy(a, b, in_sem.at[i]) for i, (a, b) in enumerate(pairs)]
    for fetch in fetches:
        fetch.start()

    lane = iota((1, LANES), 1)
    chunk = lax.shift_right_logical(lane, shift)
    for fetch in fetches[0:3]:
        fetch.wait()
    counted = jnp.zeros((1, LANES), I32)
    for o in range(devices):
        counted = jnp.where(chunk == o, counts_v[:, o : o + 1], counted)
    live = (lane & (capacity - 1)) < counted
    ids_row = jnp.where(live, blocks_v[...], -1).astype(F32)
    head[...] = jnp.zeros_like(head)
    head[0:1, 0:3] = camera_v[...]
    head_view[my_view] = head[...]

    def remote(src, dst, send, recv, target):
        return pltpu.make_async_remote_copy(
            src_ref=src, dst_ref=dst, send_sem=send, recv_sem=recv, device_id=target,
            device_id_type=pl.DeviceIdType.MESH,
        )

    fetches[3].wait()
    for tile in range(-(-param_rows // 8)):
        size = min(8, param_rows - 8 * tile)
        for i in range(tall):
            start = (tile * tall + i) * 8
            flat[start : start + size, :] = params_v[8 * tile : 8 * tile + size, i * LANES : (i + 1) * LANES]

    def param_row(row):
        return flat[pl.ds(row // 8 * tall * 8 + row % 8, tall, stride=8), :]

    def turn_of(angles):
        return camera_rotation([angles[:, i : i + 1] for i in range(3)])

    turn = turn_of(camera_v[...])
    record = geometry([param_row(i) for i in range(11)], [turn], centre_x, centre_y)[0]
    basis = harmonics(turn[2])
    for c in range(COLOURS):
        colour = 0.5 + basis[0] * param_row(11 + c)
        for i in range(1, 16):
            colour = colour + basis[i] * param_row(11 + 3 * i + c)
        record.append(colour)
    for f in range(9):
        fields[f] = record[f]
    fetches[4].wait()
    listed = visible_v[...]
    lists[0] = lax.shift_right_logical(listed, 7)
    lists[1] = listed & (LANES - 1)
    picked = [[] for _ in range(9)]
    for half in range(depth // 8):
        high = lists[0, half * 8 : half * 8 + 8, :]
        low = lists[1, half * 8 : half * 8 + 8, :]
        for f in range(9):
            value = jnp.zeros((8, LANES), F32)
            for h in range(tall):
                row = jnp.broadcast_to(fields[f, h : h + 1, :], (8, LANES))
                row = jnp.take_along_axis(row, low, axis=1, mode="promise_in_bounds")
                value = jnp.where(high == h, row, value)
            picked[f].append(value)
    picked = [jnp.concatenate(p, axis=0) for p in picked]

    per_tile = LANES // capacity
    dense = devices == 8 and per_tile == 8 and depth == 16
    body = depth + 2 if dense else depth * -(-9 // per_tile)

    def pack(values, extra, dst):
        if dense:
            for o, block in enumerate(swap_chunks(values[0:8], capacity)):
                dst[o, 0:depth, :] = block
            for half in range(2):
                last = swap_sublanes(values[8][half * 8 : half * 8 + 8], capacity)
                for o in range(devices):
                    dst[o, depth + half : depth + half + 1, :] = last[o : o + 1]
        for o in range(devices):
            dst[o, body : body + 1, :] = extra
            for t in range(0 if dense else -(-len(values) // per_tile)):
                block = None
                for j, value in enumerate(values[t * per_tile : (t + 1) * per_tile]):
                    moved = pltpu.roll(value, (j - o) * capacity % LANES, axis=1)
                    block = moved if block is None else jnp.where(chunk == j, moved, block)
                dst[o, t * depth : (t + 1) * depth, :] = block

    def unpack(src):
        if dense:
            values = swap_chunks([src[o, 0:depth, :] for o in range(devices)], capacity)
            last = [
                jnp.concatenate([src[o, depth + half : depth + half + 1, :] for o in range(devices)], axis=0)
                for half in range(2)
            ]
            return values + [jnp.concatenate([swap_sublanes(v, capacity) for v in last], axis=0)]
        values = []
        for f in range(9):
            t, j = divmod(f, per_tile)
            value = None
            for s in range(devices):
                moved = pltpu.roll(src[s, t * depth : (t + 1) * depth, :], (s - j) * capacity % LANES, axis=1)
                value = moved if value is None else jnp.where(chunk == s, moved, value)
            values.append(value)
        return values

    pack(picked, ids_row, out_msg)
    pl.semaphore_wait(barrier, devices - 1 + views - 1)
    records_out = [
        remote(out_msg.at[peer], in_msg.at[me], msg_send.at[d], msg_recv.at[d], {"space": peer})
        for d, peer in enumerate(peers)
    ]
    for copy in records_out:
        copy.start()
    cameras = [
        remote(head, head_view.at[my_view], camv_send.at[d], camv_recv.at[d], {"view": peer})
        for d, peer in enumerate(partners)
    ]
    for copy in cameras:
        copy.start()
    in_msg[me] = out_msg[me]

    def own_rows(b, sub):
        return pl.ds((MARGIN + b * 8) * subs + sub, 8, stride=subs)

    fetches[7].wait()
    for ch in range(COLOURS):
        for b in range(block_rows):
            for g in range(groups):
                goal[own_rows(b, ch * groups + g), :] = target_v[ch, b * 8 : b * 8 + 8, g * LANES : (g + 1) * LANES]

    reach = MARGIN * subs
    top, bottom = MARGIN * subs, strip_rows * subs

    def exchange(ref, send, recv):
        upward = remote(
            ref.at[pl.ds(top, reach)], ref.at[pl.ds((MARGIN + strip_rows) * subs, reach)],
            send.at[0], recv.at[0], {"space": lax.rem(me + devices - 1, devices)},
        )
        downward = remote(
            ref.at[pl.ds(bottom, reach)], ref.at[pl.ds(0, reach)],
            send.at[1], recv.at[1], {"space": lax.rem(me + 1, devices)},
        )
        return upward, downward

    not_first, not_last = me > 0, me < devices - 1

    def begin(copies):
        pl.when(not_first)(copies[0].start)
        pl.when(not_last)(copies[1].start)

    def arrived(copies):
        pl.when(not_last)(copies[0].wait_recv)
        pl.when(not_first)(copies[1].wait_recv)

    def left(copies):
        pl.when(not_first)(copies[0].wait_send)
        pl.when(not_last)(copies[1].wait_send)

    goal_copies = exchange(goal, goal_send, goal_recv)
    begin(goal_copies)

    square = (LANES, LANES)
    fetches[5].wait()
    ranks = jnp.zeros((1, LANES), I32)
    for s in range(devices):
        ranks = jnp.where(chunk == s, rank_v[:, s : s + 1], ranks)
    offset = iota(square, 1) - iota(square, 0)
    near = iota(square, 0) < LANES // 2
    beside = jnp.where(near, offset - LANES, offset + LANES)
    exact = [np.float32(tap) for tap in taps]
    highs = [float(tap.astype(jnp.bfloat16)) for tap in exact]
    lows = [float((tap - np.float32(high)).astype(jnp.bfloat16)) for tap, high in zip(exact, highs)]
    blur_norm = float(1.0 / (sum(highs) + sum(lows)))
    for side, values in enumerate((highs, lows)):
        for part, distance in enumerate((offset, beside)):
            weights = jnp.zeros(square, F32)
            for i in range(11):
                weights = jnp.where(distance == i - HALO, values[i], weights)
            weights = weights.astype(BF16)
            for term in range(3):
                start = (term * 2 + part) * LANES
                taps_w[start : start + LANES, side * LANES : (side + 1) * LANES] = weights

    slot_value = lane.astype(F32)

    def invert(k, total):
        high = lists[0, pl.ds(k, 1), :]
        low = lists[1, pl.ds(k, 1), :]
        hit = iota((tall, LANES), 0) == high
        left = jnp.concatenate(
            [jnp.where(hit, slot_value, 0.0), jnp.where(hit, k.astype(F32), 0.0)], axis=0
        ).astype(BF16)
        right = jnp.where(iota(square, 0) == low, 1.0, 0.0).astype(BF16)
        return total + lax.dot_general(left, right, NT, preferred_element_type=F32)

    inverse[...] = lax.fori_loop(0, depth, invert, jnp.zeros((2 * tall, LANES), F32)).astype(I32)

    height_px = strip_rows * devices
    mid, end = rows_mid * subs, strip_rows * subs
    for at in range(0, mid, 8):
        line = iota((8, LANES), 0) + at
        row_y = (line.astype(F32) + 0.5) * (1.0 / subs)
        y = row_y + (me * strip_rows - HALO).astype(F32)
        counts_here = (y > 0.0) & (y < float(height_px))
        seed_s[at : at + 8, :] = jnp.where(counts_here, -0.2, 0.0)
        own_s[at : at + 8, :] = jnp.where((row_y > HALO) & (row_y < HALO + strip_rows), 1.0, 0.0)

    for copy in records_out:
        copy.wait_recv()
    owned = jnp.zeros((1, LANES), F32)
    for s in range(devices):
        amount = lax.rem(s - me + devices, devices) * capacity
        owned = jnp.where(chunk == s, pltpu.roll(in_msg[s, body : body + 1, :], amount, axis=1), owned)
    own_ids = jnp.maximum(owned, 0.0)
    block_y = jnp.floor((own_ids + 0.5) * (1.0 / block_cols))
    block_x = own_ids - block_y * block_cols
    corner_x = block_x * 16.0 + 0.5
    corner_y = block_y * 8.0 + (me * strip_rows).astype(F32) + 0.5
    got = unpack(in_msg)
    rec[0] = corner_x - got[0]
    rec[1] = corner_y - got[1]
    rec[2] = -0.5 * LOG2E * got[2]
    rec[3] = -LOG2E * got[3]
    rec[4] = -0.5 * LOG2E * got[4]
    rec[5] = jnp.log2(got[5])
    for f in range(6, 9):
        rec[f] = got[f]
    for f in range(2, 6):
        rec[7 + f] = got[f]
    vreg = (8, LANES)
    rows_f = iota(vreg, 0).astype(F32)

    def wide(f, k):
        return jnp.broadcast_to(rec[f, k : k + 1, :], vreg)

    width_c = 4

    def render_some(index, carry):
        trans = [jnp.ones(vreg, F32)] * width_c
        logs = [jnp.zeros(vreg, F32)] * width_c
        run = [None] * width_c
        sums = [[jnp.zeros(vreg, F32)] * width_c for _ in range(COLOURS)]
        base = (index * width_c).astype(F32)
        for k in range(depth):
            delta_y = wide(1, k) + rows_f
            cross = wide(3, k) * delta_y
            square_y = wide(4, k) * delta_y * delta_y + wide(5, k)
            first_x = wide(0, k) + base
            curve = wide(2, k)
            tint = [wide(6 + ch, k) for ch in range(COLOURS)]
            for j in range(width_c):
                delta_x = first_x + float(j)
                alpha = jnp.exp2((curve * delta_x + cross) * delta_x + square_y)
                place = pl.ds(pl.multiple_of((index * width_c + j) * 8, 8), 8)
                alpha_s[k, place, :] = alpha
                trans_s[k, place, :] = trans[j]
                weight = alpha * trans[j]
                for ch in range(COLOURS):
                    sums[ch][j] = sums[ch][j] + weight * tint[ch]
                kept = 1.0 - alpha
                trans[j] = trans[j] * kept
                run[j] = kept if k % 4 == 0 else run[j] * kept
                if k % 4 == 3 or k == depth - 1:
                    logs[j] = logs[j] + jnp.log(run[j])
        for j in range(width_c):
            place = pl.ds(pl.multiple_of((index * width_c + j) * 8, 8), 8)
            for ch in range(COLOURS):
                seg[ch, place, :] = sums[ch][j]
            seg[3, place, :] = trans[j]
            seg[4, place, :] = logs[j]
        return carry

    lax.fori_loop(0, 16 // width_c, render_some, 0)

    diagonal = iota(square, 0) == iota(square, 1)
    ranks_f = ranks.astype(F32)
    owned_c = jnp.sum(jnp.where(diagonal, owned, 0.0), axis=1, keepdims=True)
    ranks_c = jnp.sum(jnp.where(diagonal, ranks_f, 0.0), axis=1, keepdims=True)
    same = owned_c == owned
    fwd_mask = jnp.where(same & (ranks_c < ranks_f), 1.0, 0.0).astype(BF16)
    bwd_mask = jnp.where(same & (ranks_c > ranks_f), 1.0, 0.0).astype(BF16)
    blocks_here = LANES // 2
    lane_sq, sub_sq = iota(square, 1).astype(F32), iota(square, 0).astype(F32)
    for part in range(3):
        nearer[part * LANES : (part + 1) * LANES, :] = fwd_mask
        further[part * LANES : (part + 1) * LANES, :] = bwd_mask
    for d in range(2):
        alive = owned_c >= 0.0
        forth = jnp.where(alive & (lane_sq == owned_c + d * blocks_here), 1.0, 0.0).astype(BF16)
        back = jnp.where((owned >= 0.0) & (sub_sq == owned + d * blocks_here), 1.0, 0.0).astype(BF16)
        for part in range(3):
            place_f[(part * 2 + d) * LANES : (part * 2 + d + 1) * LANES, :] = forth
            place_b[part * LANES : (part + 1) * LANES, d * LANES : (d + 1) * LANES] = back

    before = jnp.dot(
        jnp.concatenate(three_parts(seg[4]), axis=1), nearer[...], preferred_element_type=F32
    )
    seg[4] = jnp.exp(before)
    fetches[6].wait()
    backs = [backdrop_v[:, ch : ch + 1] for ch in range(COLOURS)]
    shares = [[None] * 16 for _ in range(COLOURS)]
    for c in range(16):
        part = slice(c * 8, c * 8 + 8)
        share = seg[4, part, :]
        taken = 1.0 - seg[3, part, :]
        for ch in range(COLOURS):
            tinted = seg[ch, part, :] - backs[ch] * taken
            seg[ch, part, :] = tinted
            shares[ch][c] = share * tinted
    across_lanes = iota(vreg, 1)
    to_natural = (across_lanes & 15) * 8 + lax.shift_right_logical(across_lanes, 4)
    from_natural = (across_lanes & 7) * 16 + lax.shift_right_logical(across_lanes, 3)
    for ch in range(COLOURS):
        paired = jnp.concatenate(
            [jnp.concatenate([shares[ch][c], shares[ch][c + 8]], axis=1) for c in range(8)], axis=0
        )
        placed = jnp.dot(
            jnp.concatenate(three_parts(paired), axis=1), place_f[...], preferred_element_type=F32
        )
        for q, value in enumerate(swap_chunks([placed[c * 8 : c * 8 + 8] for c in range(8)], 8)):
            b, g = divmod(q, groups)
            value = jnp.take_along_axis(value, to_natural, axis=1, mode="promise_in_bounds") + backs[ch]
            image[own_rows(b, ch * groups + g), :] = value
            picture_out[0, ch, b * 8 : b * 8 + 8, g * LANES : (g + 1) * LANES] = value
    image_copies = exchange(image, image_send, image_recv)
    begin(image_copies)

    def blur_rows(load, count, store):
        seen = {}

        def line(at):
            if at not in seen:
                seen[at] = load(at)
            return seen[at]

        for at in range(0, count * subs, 8):
            total = taps[5] * line(at + 5 * subs)
            for i in range(5):
                total = total + taps[i] * (line(at + i * subs) + line(at + (10 - i) * subs))
            store(at, total)

    def reader(ref, base=0):
        return lambda at: ref[base + at : base + at + 8, :]

    def writer(base):
        def store(at, value):
            rows_buf[8 + base + at : 16 + base + at, :] = value

        return store

    sub_group = iota((1, 8, LANES), 1) & (groups - 1)
    low_lanes = iota((1, 8, LANES), 2) < LANES // 2
    from_right = low_lanes & (sub_group < groups - 1)
    from_left = jnp.logical_not(low_lanes) & (sub_group > 0)

    def blur_columns(first, size):
        def read(at):
            return rows_buf[at : at + size, :].reshape(size // 8, 8, LANES)

        rim = jnp.where(from_right, read(first + 9), jnp.where(from_left, read(first + 7), 0.0))
        own_parts = three_parts(rows_buf[first + 8 : first + 8 + size, :])
        rim_parts = three_parts(rim.reshape(size, LANES))
        both = jnp.dot(
            jnp.concatenate([v for pair in zip(own_parts, rim_parts) for v in pair], axis=1),
            taps_w[...],
            preferred_element_type=F32,
        )
        return (both[:, 0:LANES] + both[:, LANES : 2 * LANES]) * blur_norm

    def blur_all(total, dst):
        half = -(-total // 32) * 16
        dst[0:half, :] = blur_columns(0, half)
        dst[half:total, :] = blur_columns(half, total - half)

    arrived(goal_copies)
    from_goal, from_image = reader(goal), reader(image)
    rows_buf[0:8, :] = jnp.zeros_like(rows_buf[0:8, :])
    rows_buf[8 + 3 * mid : 16 + 3 * mid, :] = jnp.zeros_like(rows_buf[0:8, :])
    blur_rows(from_goal, rows_mid, writer(0))
    blur_rows(lambda at: from_goal(at) * from_goal(at), rows_mid, writer(mid))
    blur_all(2 * mid, goal_buf)

    arrived(image_copies)
    blur_rows(from_image, rows_mid, writer(0))
    blur_rows(lambda at: from_image(at) * from_image(at), rows_mid, writer(mid))
    blur_rows(lambda at: from_image(at) * from_goal(at), rows_mid, writer(2 * mid))
    blur_all(3 * mid, cols_buf)

    step_rows = mid // 3

    def similarity(index, total):
        at = pl.multiple_of(index * step_rows, 8)

        def take(ref, base):
            return ref[pl.ds(at + base, step_rows), :]

        mean_a, raw_aa, raw_ab = take(cols_buf, 0), take(cols_buf, mid), take(cols_buf, 2 * mid)
        mean_b, raw_bb = take(goal_buf, 0), take(goal_buf, mid)
        pixel_a, pixel_b = take(image, HALO * subs), take(goal, HALO * subs)
        seed = take(seed_s, 0)
        square_a, square_b, cross = mean_a * mean_a, mean_b * mean_b, mean_a * mean_b
        first_n = 2.0 * cross + SSIM_FIRST
        second_n = 2.0 * (raw_ab - cross) + SSIM_SECOND
        first_d = square_a + square_b + SSIM_FIRST
        second_d = (raw_aa - square_a) + (raw_bb - square_b) + SSIM_SECOND
        scale = 1.0 / (first_d * second_d)
        ssim = first_n * second_n * scale
        inv_first, inv_second = second_d * scale, first_d * scale
        by_aa = -ssim * inv_second
        by_ab = 2.0 * first_n * scale
        by_a = 2.0 * (mean_b * second_n * scale - mean_a * (ssim * inv_first + by_aa)) - mean_b * by_ab
        adj[pl.ds(at, step_rows), :] = seed * by_a
        adj[pl.ds(at + mid, step_rows), :] = seed * by_aa
        adj[pl.ds(at + 2 * mid, step_rows), :] = seed * by_ab
        differ = pixel_a - pixel_b
        term = 0.8 * jnp.sqrt(differ * differ + SMOOTHING) + 0.2 * (1.0 - ssim)
        return total + term * take(own_s, 0)

    own_terms = lax.fori_loop(0, 3, similarity, jnp.zeros((step_rows, LANES), F32))
    own_loss = jnp.sum(jnp.sum(own_terms, axis=1, keepdims=True), axis=0, keepdims=True)

    for q in range(3):
        blur_rows(reader(adj, q * mid), strip_rows, writer(q * end))
    blur_all(3 * end, cols_buf)
    pixel_a = image[MARGIN * subs : MARGIN * subs + end, :]
    pixel_b = goal[MARGIN * subs : MARGIN * subs + end, :]
    differ = pixel_a - pixel_b
    adj[0:end, :] = (
        cols_buf[0:end, :]
        + 2.0 * pixel_a * cols_buf[end : 2 * end, :]
        + pixel_b * cols_buf[2 * end : 3 * end, :]
        + 0.8 * differ * lax.rsqrt(differ * differ + SMOOTHING)
    )

    pulled = []
    for ch in range(COLOURS):
        bands_here = []
        for q in range(bands):
            b, g = divmod(q, groups)
            value = adj[pl.ds(b * 8 * subs + ch * groups + g, 8, stride=subs), :]
            bands_here.append(jnp.take_along_axis(value, from_natural, axis=1, mode="promise_in_bounds"))
        pulled.append(
            jnp.dot(
                jnp.concatenate(three_parts(jnp.concatenate(swap_chunks(bands_here, 8), axis=0)), axis=1),
                place_b[...],
                preferred_element_type=F32,
            )
        )
    for c in range(16):
        part = slice(c * 8, c * 8 + 8)
        share = seg[4, part, :]
        by_share, by_trans = None, None
        for ch in range(COLOURS):
            grad = pulled[ch][c % 8 * 8 : c % 8 * 8 + 8, c // 8 * LANES : (c // 8 + 1) * LANES]
            piece = grad * seg[ch, part, :]
            by_share = piece if by_share is None else by_share + piece
            grad = grad * share
            seg[ch, part, :] = grad
            piece = grad * backs[ch]
            by_trans = piece if by_trans is None else by_trans + piece
        rows_buf[part, :] = by_share * share
        cols_buf[part, :] = by_trans
    by_log = jnp.dot(
        jnp.concatenate(three_parts(rows_buf[0:LANES, :]), axis=1), further[...], preferred_element_type=F32
    )
    trans = seg[3]
    visible_through = trans > 2e-38
    cols_buf[0:LANES, :] += jnp.where(visible_through, by_log / jnp.where(visible_through, trans, 1.0), 0.0)

    def unrender(step, carry):
        k = depth - 1 - step
        row = pl.ds(k, 1)

        def across(f):
            return jnp.broadcast_to(rec[f, row, :], vreg)

        delta_y = across(1) + rows_f
        first_x = across(0)
        tint = [across(6 + ch) for ch in range(COLOURS)]
        sums = [jnp.zeros(vreg, F32)] * 6
        for c in range(16):
            part = slice(c * 8, c * 8 + 8)
            alpha = alpha_s[k, part, :]
            weight = alpha * trans_s[k, part, :]
            behind = cols_buf[part, :]
            grads = [seg[ch, part, :] for ch in range(COLOURS)]
            gap = grads[0] * tint[0] + grads[1] * tint[1] + grads[2] * tint[2] - behind
            cols_buf[part, :] = behind + alpha * gap
            slope = weight * gap
            delta_x = first_x + float(c)
            slope_x = slope * delta_x
            terms = [slope, slope_x, slope_x * delta_x] + [weight * g for g in grads]
            sums = [a + b for a, b in zip(sums, terms)]
        rows = [
            sums[0], sums[1], sums[0] * delta_y, sums[2], sums[1] * delta_y, sums[0] * delta_y * delta_y,
            sums[3], sums[4], sums[5],
        ]
        for f, value in enumerate(rows):
            moments[f, row, :] = jnp.sum(value, axis=0, keepdims=True)
        return carry

    lax.fori_loop(0, depth, unrender, 0)
    conic_a, conic_b, conic_c, opaque = [rec[9 + i] for i in range(4)]
    grads_out = [
        conic_a * moments[1] + conic_b * moments[2],
        conic_b * moments[1] + conic_c * moments[2],
        -0.5 * moments[3],
        -moments[4],
        -0.5 * moments[5],
        moments[0] / opaque,
        moments[6],
        moments[7],
        moments[8],
    ]
    pack(grads_out, jnp.broadcast_to(own_loss, (1, LANES)), ret_out)
    grads_back = [
        remote(ret_out.at[peer], ret_in.at[me], ret_send.at[d], ret_recv.at[d], {"space": peer})
        for d, peer in enumerate(peers)
    ]
    for copy in grads_back:
        copy.start()
    ret_in[me] = ret_out[me]

    for copy in cameras:
        copy.wait_recv()
    for v in range(views):
        turned = turn_of(head_view[v, 0:1, :])
        for i, value in enumerate([x for row in turned for x in row] + harmonics(turned[2])):
            table_out[v, i : i + 1, :] = jnp.broadcast_to(value, (1, LANES))
    for copy in grads_back:
        copy.wait_recv()

    for f, value in enumerate(unpack(ret_in)):
        fields[f] = value
    total_loss = jnp.zeros((1, 1), F32)
    for s in range(devices):
        total_loss = total_loss + ret_in[s, body : body + 1, 0:1]
    loss_out[...] = total_loss / (3.0 * height_px * width_px)
    pair, across_x = my_view ^ 1, my_view ^ 2

    def forward(block, chunk_at, kind, target):
        piece = view_grads.at[block, pl.ds(chunk_at * 3, 3)]
        return remote(piece, piece, view_send.at[kind * 3 + chunk_at], view_recv.at[kind * 3 + chunk_at], {"view": target})

    views_out = []
    for third in range(3):
        for half in range(tall // 8):
            slot_of = inverse[half * 8 : half * 8 + 8, :]
            entry_of = inverse[tall + half * 8 : tall + half * 8 + 8, :]
            for f in range(third * 3, third * 3 + 3):
                value = jnp.zeros(vreg, F32)
                for h in range(depth):
                    row = jnp.broadcast_to(fields[f, h : h + 1, :], vreg)
                    row = jnp.take_along_axis(row, slot_of, axis=1, mode="promise_in_bounds")
                    value = jnp.where(entry_of == h, row, value)
                view_grads[my_view, f, half * 8 : half * 8 + 8, :] = value
        for kind, target in ((1, across_x), (0, pair)):
            views_out.append(forward(my_view, third, kind, target))
            views_out[-1].start()
    for third in range(3):
        forward(across_x, third, 1, across_x).wait_recv()
        views_out.append(forward(across_x, third, 2, pair))
        views_out[-1].start()
    for third in range(3):
        forward(pair, third, 0, pair).wait_recv()
        forward(my_view ^ 3, third, 2, pair).wait_recv()
    for copy in cameras + records_out + grads_back + views_out:
        copy.wait_send()
    left(goal_copies)
    left(image_copies)


def finish_kernel(sizes, params_ref, grads_ref, table_ref, picture_ref, grad_out, picture_out, flat):
    views, splats, centre_x, centre_y = sizes
    param_rows = params_ref.shape[0]
    tall = splats // LANES
    for tile in range(-(-param_rows // 8)):
        size = min(8, param_rows - 8 * tile)
        for i in range(tall) if tile < 2 else ():
            start = (tile * tall + i) * 8
            flat[start : start + size, :] = params_ref[8 * tile : 8 * tile + size, i * LANES : (i + 1) * LANES]

    def place(row):
        return pl.ds(row // 8 * tall * 8 + row % 8, tall, stride=8)

    turns = [[[table_ref[v, r * 3 + c : r * 3 + c + 1, :] for c in range(3)] for r in range(3)] for v in range(views)]
    bases = [[table_ref[v, 9 + i : 10 + i, :] for i in range(16)] for v in range(views)]
    rows = [flat[place(i), :] for i in range(11)]
    pull = jax.vjp(lambda r: geometry(r, turns, centre_x, centre_y), rows)[1]
    for i, value in enumerate(pull([[grads_ref[v, f] for f in range(6)] for v in range(views)])[0]):
        flat[place(i), :] = value
    for c in range(COLOURS):
        by_colour = [grads_ref[v, 6 + c] for v in range(views)]
        for i in range(16):
            value = bases[0][i] * by_colour[0]
            for v in range(1, views):
                value = value + bases[v][i] * by_colour[v]
            flat[place(11 + 3 * i + c), :] = value
    for tile in range(-(-param_rows // 8)):
        size = min(8, param_rows - 8 * tile)
        for i in range(tall):
            start = (tile * tall + i) * 8
            grad_out[8 * tile : 8 * tile + size, i * LANES : (i + 1) * LANES] = flat[start : start + size, :]
    picture_out[...] = picture_ref[...]


def shards(params, visible, blocks, counts, depth_rank, camera, background, target):
    devices, views = lax.axis_size("space"), lax.axis_size("view")
    slots, depth = visible.shape[1:]
    capacity = slots // devices
    strip_rows, width_px = target.shape[2:]
    splats = params.shape[1]
    tall = splats // LANES
    subs = COLOURS * (width_px // LANES)
    rows_in, rows_mid = strip_rows + 4 * HALO, strip_rows + 2 * HALO
    sizes = (devices, views, depth, slots, capacity, strip_rows, width_px, splats)
    per_tile = LANES // capacity
    dense = devices == 8 and per_tile == 8 and depth == 16
    message = (depth + 2 if dense else depth * -(-9 // per_tile)) + 1
    vmem = lambda *shape: pltpu.VMEM(shape, F32)
    half = lambda *shape: pltpu.VMEM(shape, BF16)
    dma = lambda count: pltpu.SemaphoreType.DMA((count,))
    scratch = [
        vmem(*params.shape), pltpu.VMEM((depth, slots), I32), pltpu.VMEM(blocks.shape, I32),
        pltpu.VMEM(counts.shape, I32), pltpu.VMEM(depth_rank.shape, I32), vmem(*camera.shape),
        vmem(*background.shape), vmem(*target.shape[1:]),
        vmem(-(-params.shape[0] // 8) * tall * 8, LANES), vmem(9, tall, LANES), pltpu.VMEM((2, depth, LANES), I32),
        vmem(8, LANES), vmem(views, 8, LANES),
        vmem(devices, message, LANES), vmem(devices, message, LANES),
        vmem(devices, message, LANES), vmem(devices, message, LANES),
        vmem(13, depth, LANES), half(6 * LANES, LANES), half(3 * LANES, 2 * LANES),
        half(3 * LANES, LANES), half(3 * LANES, LANES),
        half(6 * LANES, 2 * LANES), pltpu.VMEM((2 * tall, LANES), I32),
        vmem(depth, LANES, LANES), vmem(depth, LANES, LANES), vmem(5, LANES, LANES),
        vmem(rows_in * subs, LANES), vmem(rows_in * subs, LANES),
        vmem(3 * rows_mid * subs + 16, LANES), vmem(2 * rows_mid * subs, LANES), vmem(3 * rows_mid * subs, LANES),
        vmem(3 * rows_mid * subs, LANES), vmem(rows_mid * subs, LANES), vmem(rows_mid * subs, LANES),
        vmem(9, depth, LANES),
        dma(8), dma(views), dma(views), dma(devices), dma(devices), dma(devices),
        dma(devices), dma(2), dma(2), dma(2), dma(2), dma(9), dma(9),
    ]
    whole = pl.BlockSpec(memory_space=pltpu.VMEM)
    grads, table, picture, loss = pl.pallas_call(
        functools.partial(step_kernel, sizes),
        name="step",
        out_shape=(
            jax.ShapeDtypeStruct((views, 9, tall, LANES), F32),
            jax.ShapeDtypeStruct((views, TABLE, LANES), F32),
            jax.ShapeDtypeStruct(target.shape, F32),
            jax.ShapeDtypeStruct((1, 1), F32),
        ),
        in_specs=[pl.BlockSpec(memory_space=pltpu.HBM)] * 8,
        out_specs=(whole,) * 4,
        scratch_shapes=scratch,
        compiler_params=pltpu.CompilerParams(
            collective_id=0, has_side_effects=True, vmem_limit_bytes=20 * 1024 * 1024
        ),
    )(*[pltpu.with_memory_space_constraint(x, pltpu.HBM) for x in (params, jnp.swapaxes(visible, 1, 2), blocks, counts, depth_rank, camera, background, target)])
    centre = (0.5 * width_px, 0.5 * strip_rows * devices)
    grad, picture = pl.pallas_call(
        functools.partial(finish_kernel, (views, splats, *centre)),
        name="finish",
        out_shape=(jax.ShapeDtypeStruct(params.shape, F32), jax.ShapeDtypeStruct(target.shape, F32)),
        in_specs=[whole] * 4,
        out_specs=(whole,) * 2,
        scratch_shapes=[vmem(-(-params.shape[0] // 8) * tall * 8, LANES)],
        compiler_params=pltpu.CompilerParams(vmem_limit_bytes=20 * 1024 * 1024),
    )(params, grads, table, picture)
    return (grad, picture, loss.reshape(1))


def solution(mesh):
    in_specs = (
        P(None, "space"),
        P("space", None, None),
        P("space", None),
        P("space", None),
        P("view", None),
        P("view", None),
        P("view", None),
        P("view", None, "space", None),
    )
    out_specs = (P(None, "space"), P("view", None, "space", None), P("view"))
    return jax.shard_map(shards, mesh=mesh, in_specs=in_specs, out_specs=out_specs, check_vma=False)
```

time: 45.7 us -> 33.5 us (0.73)
  Pallas kernels: 38.9 us -> 30.9 us
  local copies, waits for them, and re-layouts: 3.98 us -> 0.01 us
    pallas_call x1, Pallas kernels: 38.9 us -> 29.8 us  [shards(): pl.pallas_call(functools.partial(step_kernel, sizes), name='step', out_sh...]
    unnamed x5 -> x2, local copies, waits for them, and re-layouts: 3.98 us -> 0.01 us
    pallas_call x0 -> x1, Pallas kernels: none -> 1.18 us  [shards(): pl.pallas_call(functools.partial(finish_kernel, (views, splats, *centre))...]
where the time goes in v2:
time: 33.5 us; the launch traced here: 33.4 us
  Pallas kernels  30.9 us (92%)
  between operations  2.42 us (7%)
    pallas_call x1, Pallas kernels, shards(): pl.pallas_call(functools.partial(step_kernel, sizes), name='step', out_sh...  29.8 us
    pallas_call x1, Pallas kernels, shards(): pl.pallas_call(functools.partial(finish_kernel, (views, splats, *centre))...  1.18 us

profile of v2, /device:TPU:0, one launch (start us, length us, event | category | flops | bytes accessed | tf_op | source)
XLA Modules:
  0.0 33.4 jit_solution(9866607978761452337)
XLA Ops:
  0.6 0.0 copy-start
  0.6 29.8 %step.1 = (f32[4,9,16,128]{3,2,1,0:T(8,128)S(1)}, f32[4,32,128]{2,1,0:T(8,128)S(1)}, f32[1,3,16,512]{3,2,1,0:T(8,128)S(1)}, f32[1,1]{1,0:T(1,128)}) custom-call(f32[59,2048]{1,0:T(8,128)} %params_ref.1, s32[1,16,128]{2,1,0:T(8,128)} %bitcast.2, s32[1,128]{1,0:T(1,128)} %blocks_hbm.1, s32[1,8]{1,0:T(1,128)} %counts_hbm.1, s32[1,8]{1,0:T(1,128)} %rank_hbm.1, ...), custom_call_target="tpu_custom_call" | custom-call | tf_op jit(solution)/shard_map/step/pallas_call | solution.py:853
  30.4 0.0 copy-done
  30.4 1.2 %finish.1 = (f32[59,2048]{1,0:T(8,128)}, f32[1,3,16,512]{3,2,1,0:T(8,128)}) custom-call(f32[59,2048]{1,0:T(8,128)S(1)} %copy-done, f32[4,9,16,128]{3,2,1,0:T(8,128)S(1)} %get-tuple-element.9.grads_ref, f32[4,32,128]{2,1,0:T(8,128)S(1)} %get-tuple-element.10.table_ref, f32[1,3,16,512]{3,2,1,0:T(8,128)S(1)} %get-tuple-element.11.picture_ref), custom_call_target="tpu_custom_call" | custom-call | tf_op jit(solution)/shard_map/finish/pallas_call | solution.py:870
Async XLA Ops:
  0.6 29.8 %copy-start = (f32[59,2048]{1,0:T(8,128)S(1)}, f32[59,2048]{1,0:T(8,128)}, u32[]{:S(2)}) copy-start(f32[59,2048]{1,0:T(8,128)} %params_ref.1) | copy-start | bytes 1449988

commit v3 on v2

--- a/solution.py
+++ b/solution.py
@@ -189,7 +189,6 @@
     block_cols = width_px // 16
     block_rows = strip_rows // 8
     groups = width_px // LANES
-    subs = COLOURS * groups
     bands = block_rows * groups
     rows_in = strip_rows + 4 * HALO
     rows_mid = strip_rows + 2 * HALO
@@ -197,16 +196,15 @@
     centre_y = 0.5 * strip_rows * devices
     shift = capacity.bit_length() - 1
     taps = blur_taps()
-    peers = [lax.rem(me + d, devices) for d in range(1, devices)]
-    partners = [lax.rem(my_view + d, views) for d in range(1, views)]
+    peers = [me ^ d for d in range(devices - 1, 0, -1)]
+    partners = [my_view ^ d for d in range(1, views)]
+    pair, across_x = my_view ^ 1, my_view ^ 2
 
     barrier = pltpu.get_barrier_semaphore()
-    goal[...] = jnp.zeros_like(goal)
-    image[...] = jnp.zeros_like(image)
-    for peer in peers:
-        pl.semaphore_signal(barrier, inc=1, device_id={"space": peer}, device_id_type=pl.DeviceIdType.MESH)
-    for peer in partners:
-        pl.semaphore_signal(barrier, inc=1, device_id={"view": peer}, device_id_type=pl.DeviceIdType.MESH)
+    greeted = [{"space": peer, "view": view} for peer in peers for view in (my_view, across_x)]
+    greeted += [{"space": me, "view": view} for view in partners]
+    for target in greeted:
+        pl.semaphore_signal(barrier, inc=1, device_id=target, device_id_type=pl.DeviceIdType.MESH)
     pairs = [
         (blocks_hbm, blocks_v), (counts_hbm, counts_v), (camera_hbm, camera_v), (params_hbm, params_v),
         (visible_hbm.at[0], visible_v), (rank_hbm, rank_v), (backdrop_hbm, backdrop_v), (target_hbm.at[0], target_v),
@@ -214,6 +212,19 @@
     fetches = [pltpu.make_async_copy(a, b, in_sem.at[i]) for i, (a, b) in enumerate(pairs)]
     for fetch in fetches:
         fetch.start()
+
+    rim = MARGIN * groups
+
+    @pl.when(me == 0)
+    def _():
+        goal[:, 0:rim, :] = jnp.zeros((COLOURS, rim, LANES), F32)
+        image[:, 0:rim, :] = jnp.zeros((COLOURS, rim, LANES), F32)
+
+    @pl.when(me == devices - 1)
+    def _():
+        low = (MARGIN + strip_rows) * groups
+        goal[:, low : low + rim, :] = jnp.zeros((COLOURS, rim, LANES), F32)
+        image[:, low : low + rim, :] = jnp.zeros((COLOURS, rim, LANES), F32)
 
     lane = iota((1, LANES), 1)
     chunk = lax.shift_right_logical(lane, shift)
@@ -314,7 +325,7 @@
         return values
 
     pack(picked, ids_row, out_msg)
-    pl.semaphore_wait(barrier, devices - 1 + views - 1)
+    pl.semaphore_wait(barrier, len(greeted))
     records_out = [
         remote(out_msg.at[peer], in_msg.at[me], msg_send.at[d], msg_recv.at[d], {"space": peer})
         for d, peer in enumerate(peers)
@@ -329,26 +340,25 @@
         copy.start()
     in_msg[me] = out_msg[me]
 
-    def own_rows(b, sub):
-        return pl.ds((MARGIN + b * 8) * subs + sub, 8, stride=subs)
+    def own_rows(b, g):
+        return pl.ds((MARGIN + b * 8) * groups + g, 8, stride=groups)
 
     fetches[7].wait()
     for ch in range(COLOURS):
         for b in range(block_rows):
             for g in range(groups):
-                goal[own_rows(b, ch * groups + g), :] = target_v[ch, b * 8 : b * 8 + 8, g * LANES : (g + 1) * LANES]
-
-    reach = MARGIN * subs
-    top, bottom = MARGIN * subs, strip_rows * subs
-
-    def exchange(ref, send, recv):
+                goal[ch, own_rows(b, g), :] = target_v[ch, b * 8 : b * 8 + 8, g * LANES : (g + 1) * LANES]
+
+    top, bottom, below = MARGIN * groups, strip_rows * groups, (MARGIN + strip_rows) * groups
+
+    def exchange(ref, channels, send, recv, at):
         upward = remote(
-            ref.at[pl.ds(top, reach)], ref.at[pl.ds((MARGIN + strip_rows) * subs, reach)],
-            send.at[0], recv.at[0], {"space": lax.rem(me + devices - 1, devices)},
+            ref.at[channels, pl.ds(top, rim)], ref.at[channels, pl.ds(below, rim)],
+            send.at[at], recv.at[at], {"space": lax.rem(me + devices - 1, devices)},
         )
         downward = remote(
-            ref.at[pl.ds(bottom, reach)], ref.at[pl.ds(0, reach)],
-            send.at[1], recv.at[1], {"space": lax.rem(me + 1, devices)},
+            ref.at[channels, pl.ds(bottom, rim)], ref.at[channels, pl.ds(0, rim)],
+            send.at[at + 1], recv.at[at + 1], {"space": lax.rem(me + 1, devices)},
         )
         return upward, downward
 
@@ -366,7 +376,7 @@
         pl.when(not_first)(copies[0].wait_send)
         pl.when(not_last)(copies[1].wait_send)
 
-    goal_copies = exchange(goal, goal_send, goal_recv)
+    goal_copies = exchange(goal, slice(None), goal_send, goal_recv, 0)
     begin(goal_copies)
 
     square = (LANES, LANES)
@@ -406,10 +416,10 @@
     inverse[...] = lax.fori_loop(0, depth, invert, jnp.zeros((2 * tall, LANES), F32)).astype(I32)
 
     height_px = strip_rows * devices
-    mid, end = rows_mid * subs, strip_rows * subs
+    mid, end = rows_mid * groups, strip_rows * groups
     for at in range(0, mid, 8):
         line = iota((8, LANES), 0) + at
-        row_y = (line.astype(F32) + 0.5) * (1.0 / subs)
+        row_y = (line.astype(F32) + 0.5) * (1.0 / groups)
         y = row_y + (me * strip_rows - HALO).astype(F32)
         counts_here = (y > 0.0) & (y < float(height_px))
         seed_s[at : at + 8, :] = jnp.where(counts_here, -0.2, 0.0)
@@ -520,6 +530,7 @@
     across_lanes = iota(vreg, 1)
     to_natural = (across_lanes & 15) * 8 + lax.shift_right_logical(across_lanes, 4)
     from_natural = (across_lanes & 7) * 16 + lax.shift_right_logical(across_lanes, 3)
+    image_copies = []
     for ch in range(COLOURS):
         paired = jnp.concatenate(
             [jnp.concatenate([shares[ch][c], shares[ch][c + 8]], axis=1) for c in range(8)], axis=0
@@ -530,10 +541,10 @@
         for q, value in enumerate(swap_chunks([placed[c * 8 : c * 8 + 8] for c in range(8)], 8)):
             b, g = divmod(q, groups)
             value = jnp.take_along_axis(value, to_natural, axis=1, mode="promise_in_bounds") + backs[ch]
-            image[own_rows(b, ch * groups + g), :] = value
+            image[ch, own_rows(b, g), :] = value
             picture_out[0, ch, b * 8 : b * 8 + 8, g * LANES : (g + 1) * LANES] = value
-    image_copies = exchange(image, image_send, image_recv)
-    begin(image_copies)
+        image_copies.append(exchange(image, ch, image_send, image_recv, 2 * ch))
+        begin(image_copies[ch])
 
     def blur_rows(load, count, store):
         seen = {}
@@ -543,14 +554,14 @@
                 seen[at] = load(at)
             return seen[at]
 
-        for at in range(0, count * subs, 8):
-            total = taps[5] * line(at + 5 * subs)
+        for at in range(0, count * groups, 8):
+            total = taps[5] * line(at + 5 * groups)
             for i in range(5):
-                total = total + taps[i] * (line(at + i * subs) + line(at + (10 - i) * subs))
+                total = total + taps[i] * (line(at + i * groups) + line(at + (10 - i) * groups))
             store(at, total)
 
-    def reader(ref, base=0):
-        return lambda at: ref[base + at : base + at + 8, :]
+    def reader(ref, ch):
+        return lambda at: ref[ch, at : at + 8, :]
 
     def writer(base):
         def store(at, value):
@@ -563,51 +574,47 @@
     from_right = low_lanes & (sub_group < groups - 1)
     from_left = jnp.logical_not(low_lanes) & (sub_group > 0)
 
-    def blur_columns(first, size):
+    def blur_columns(first, size, terms):
         def read(at):
             return rows_buf[at : at + size, :].reshape(size // 8, 8, LANES)
 
-        rim = jnp.where(from_right, read(first + 9), jnp.where(from_left, read(first + 7), 0.0))
-        own_parts = three_parts(rows_buf[first + 8 : first + 8 + size, :])
-        rim_parts = three_parts(rim.reshape(size, LANES))
+        sides = jnp.where(from_right, read(first + 9), jnp.where(from_left, read(first + 7), 0.0))
+        own_parts = three_parts(rows_buf[first + 8 : first + 8 + size, :])[0:terms]
+        rim_parts = three_parts(sides.reshape(size, LANES))[0:terms]
         both = jnp.dot(
             jnp.concatenate([v for pair in zip(own_parts, rim_parts) for v in pair], axis=1),
-            taps_w[...],
+            taps_w[0 : terms * 2 * LANES, :],
             preferred_element_type=F32,
         )
         return (both[:, 0:LANES] + both[:, LANES : 2 * LANES]) * blur_norm
 
-    def blur_all(total, dst):
+    def blur_all(total, dst, terms=3):
         half = -(-total // 32) * 16
-        dst[0:half, :] = blur_columns(0, half)
-        dst[half:total, :] = blur_columns(half, total - half)
-
+        dst[0:half, :] = blur_columns(0, half, terms)
+        dst[half:total, :] = blur_columns(half, total - half, terms)
+
+    rows_buf[0:8, :] = jnp.zeros_like(rows_buf[0:8, :])
+    rows_buf[8 + 6 * mid : 16 + 6 * mid, :] = jnp.zeros_like(rows_buf[0:8, :])
     arrived(goal_copies)
-    from_goal, from_image = reader(goal), reader(image)
-    rows_buf[0:8, :] = jnp.zeros_like(rows_buf[0:8, :])
-    rows_buf[8 + 3 * mid : 16 + 3 * mid, :] = jnp.zeros_like(rows_buf[0:8, :])
-    blur_rows(from_goal, rows_mid, writer(0))
-    blur_rows(lambda at: from_goal(at) * from_goal(at), rows_mid, writer(mid))
-    blur_all(2 * mid, goal_buf)
-
-    arrived(image_copies)
-    blur_rows(from_image, rows_mid, writer(0))
-    blur_rows(lambda at: from_image(at) * from_image(at), rows_mid, writer(mid))
-    blur_rows(lambda at: from_image(at) * from_goal(at), rows_mid, writer(2 * mid))
-    blur_all(3 * mid, cols_buf)
-
-    step_rows = mid // 3
-
-    def similarity(index, total):
-        at = pl.multiple_of(index * step_rows, 8)
-
-        def take(ref, base):
-            return ref[pl.ds(at + base, step_rows), :]
-
-        mean_a, raw_aa, raw_ab = take(cols_buf, 0), take(cols_buf, mid), take(cols_buf, 2 * mid)
-        mean_b, raw_bb = take(goal_buf, 0), take(goal_buf, mid)
-        pixel_a, pixel_b = take(image, HALO * subs), take(goal, HALO * subs)
-        seed = take(seed_s, 0)
+    for ch in range(COLOURS):
+        from_goal = reader(goal, ch)
+        blur_rows(from_goal, rows_mid, writer(2 * ch * mid))
+        blur_rows(lambda at: from_goal(at) * from_goal(at), rows_mid, writer((2 * ch + 1) * mid))
+    blur_all(6 * mid, goal_buf)
+
+    own_terms, pulled = None, []
+    for ch in range(COLOURS):
+        arrived(image_copies[ch])
+        from_goal, from_image = reader(goal, ch), reader(image, ch)
+        blur_rows(from_image, rows_mid, writer(0))
+        blur_rows(lambda at: from_image(at) * from_image(at), rows_mid, writer(mid))
+        blur_rows(lambda at: from_image(at) * from_goal(at), rows_mid, writer(2 * mid))
+        blur_all(3 * mid, cols_buf)
+        mean_a, raw_aa, raw_ab = (cols_buf[q * mid : (q + 1) * mid, :] for q in range(3))
+        mean_b, raw_bb = (goal_buf[(2 * ch + q) * mid : (2 * ch + q + 1) * mid, :] for q in range(2))
+        centre_rows = slice(HALO * groups, HALO * groups + mid)
+        pixel_a, pixel_b = image[ch, centre_rows, :], goal[ch, centre_rows, :]
+        seed = seed_s[...]
         square_a, square_b, cross = mean_a * mean_a, mean_b * mean_b, mean_a * mean_b
         first_n = 2.0 * cross + SSIM_FIRST
         second_n = 2.0 * (raw_ab - cross) + SSIM_SECOND
@@ -619,35 +626,28 @@
         by_aa = -ssim * inv_second
         by_ab = 2.0 * first_n * scale
         by_a = 2.0 * (mean_b * second_n * scale - mean_a * (ssim * inv_first + by_aa)) - mean_b * by_ab
-        adj[pl.ds(at, step_rows), :] = seed * by_a
-        adj[pl.ds(at + mid, step_rows), :] = seed * by_aa
-        adj[pl.ds(at + 2 * mid, step_rows), :] = seed * by_ab
+        adj[0, 0:mid, :] = seed * by_a
+        adj[1, 0:mid, :] = seed * by_aa
+        adj[2, 0:mid, :] = seed * by_ab
         differ = pixel_a - pixel_b
-        term = 0.8 * jnp.sqrt(differ * differ + SMOOTHING) + 0.2 * (1.0 - ssim)
-        return total + term * take(own_s, 0)
-
-    own_terms = lax.fori_loop(0, 3, similarity, jnp.zeros((step_rows, LANES), F32))
-    own_loss = jnp.sum(jnp.sum(own_terms, axis=1, keepdims=True), axis=0, keepdims=True)
-
-    for q in range(3):
-        blur_rows(reader(adj, q * mid), strip_rows, writer(q * end))
-    blur_all(3 * end, cols_buf)
-    pixel_a = image[MARGIN * subs : MARGIN * subs + end, :]
-    pixel_b = goal[MARGIN * subs : MARGIN * subs + end, :]
-    differ = pixel_a - pixel_b
-    adj[0:end, :] = (
-        cols_buf[0:end, :]
-        + 2.0 * pixel_a * cols_buf[end : 2 * end, :]
-        + pixel_b * cols_buf[2 * end : 3 * end, :]
-        + 0.8 * differ * lax.rsqrt(differ * differ + SMOOTHING)
-    )
-
-    pulled = []
-    for ch in range(COLOURS):
+        term = (0.8 * jnp.sqrt(differ * differ + SMOOTHING) + 0.2 * (1.0 - ssim)) * own_s[...]
+        own_terms = term if own_terms is None else own_terms + term
+        for q in range(3):
+            blur_rows(reader(adj, q), strip_rows, writer(q * end))
+        blur_all(3 * end, cols_buf, terms=2)
+        own_pixels = slice(MARGIN * groups, MARGIN * groups + end)
+        pixel_a, pixel_b = image[ch, own_pixels, :], goal[ch, own_pixels, :]
+        differ = pixel_a - pixel_b
+        adj[0, 0:end, :] = (
+            cols_buf[0:end, :]
+            + 2.0 * pixel_a * cols_buf[end : 2 * end, :]
+            + pixel_b * cols_buf[2 * end : 3 * end, :]
+            + 0.8 * differ * lax.rsqrt(differ * differ + SMOOTHING)
+        )
         bands_here = []
         for q in range(bands):
             b, g = divmod(q, groups)
-            value = adj[pl.ds(b * 8 * subs + ch * groups + g, 8, stride=subs), :]
+            value = adj[0, pl.ds(b * 8 * groups + g, 8, stride=groups), :]
             bands_here.append(jnp.take_along_axis(value, from_natural, axis=1, mode="promise_in_bounds"))
         pulled.append(
             jnp.dot(
@@ -656,6 +656,8 @@
                 preferred_element_type=F32,
             )
         )
+    own_loss = jnp.sum(jnp.sum(own_terms, axis=1, keepdims=True), axis=0, keepdims=True)
+
     for c in range(16):
         part = slice(c * 8, c * 8 + 8)
         share = seg[4, part, :]
@@ -724,12 +726,19 @@
     ]
     pack(grads_out, jnp.broadcast_to(own_loss, (1, LANES)), ret_out)
     grads_back = [
-        remote(ret_out.at[peer], ret_in.at[me], ret_send.at[d], ret_recv.at[d], {"space": peer})
+        remote(ret_out.at[peer], ret_in.at[0, me], ret_send.at[d], ret_recv.at[d], {"space": peer})
         for d, peer in enumerate(peers)
     ]
-    for copy in grads_back:
+    grads_across = [
+        remote(
+            ret_out.at[peer], ret_in.at[1, me], ret_send.at[devices + d], ret_recv.at[devices + d],
+            {"space": peer, "view": across_x},
+        )
+        for d, peer in enumerate(peers + [me])
+    ]
+    for copy in grads_across + grads_back:
         copy.start()
-    ret_in[me] = ret_out[me]
+    ret_in[0, me] = ret_out[me]
 
     for copy in cameras:
         copy.wait_recv()
@@ -737,53 +746,56 @@
         turned = turn_of(head_view[v, 0:1, :])
         for i, value in enumerate([x for row in turned for x in row] + harmonics(turned[2])):
             table_out[v, i : i + 1, :] = jnp.broadcast_to(value, (1, LANES))
-    for copy in grads_back:
-        copy.wait_recv()
-
-    for f, value in enumerate(unpack(ret_in)):
-        fields[f] = value
-    total_loss = jnp.zeros((1, 1), F32)
-    for s in range(devices):
-        total_loss = total_loss + ret_in[s, body : body + 1, 0:1]
-    loss_out[...] = total_loss / (3.0 * height_px * width_px)
-    pair, across_x = my_view ^ 1, my_view ^ 2
-
-    def forward(block, chunk_at, kind, target):
-        piece = view_grads.at[block, pl.ds(chunk_at * 3, 3)]
-        return remote(piece, piece, view_send.at[kind * 3 + chunk_at], view_recv.at[kind * 3 + chunk_at], {"view": target})
 
     views_out = []
-    for third in range(3):
+    for which, (view, waits) in enumerate(((across_x, grads_across), (my_view, grads_back))):
+        for copy in waits:
+            copy.wait_recv()
+        for f, value in enumerate(unpack(ret_in.at[1 - which])):
+            fields[f] = value
         for half in range(tall // 8):
             slot_of = inverse[half * 8 : half * 8 + 8, :]
             entry_of = inverse[tall + half * 8 : tall + half * 8 + 8, :]
-            for f in range(third * 3, third * 3 + 3):
+            for f in range(9):
                 value = jnp.zeros(vreg, F32)
                 for h in range(depth):
                     row = jnp.broadcast_to(fields[f, h : h + 1, :], vreg)
                     row = jnp.take_along_axis(row, slot_of, axis=1, mode="promise_in_bounds")
                     value = jnp.where(entry_of == h, row, value)
-                view_grads[my_view, f, half * 8 : half * 8 + 8, :] = value
-        for kind, target in ((1, across_x), (0, pair)):
-            views_out.append(forward(my_view, third, kind, target))
-            views_out[-1].start()
-    for third in range(3):
-        forward(across_x, third, 1, across_x).wait_recv()
-        views_out.append(forward(across_x, third, 2, pair))
-        views_out[-1].start()
-    for third in range(3):
-        forward(pair, third, 0, pair).wait_recv()
-        forward(my_view ^ 3, third, 2, pair).wait_recv()
-    for copy in cameras + records_out + grads_back + views_out:
+                view_grads[view, f, half * 8 : half * 8 + 8, :] = value
+        piece = view_grads.at[view]
+        views_out.append(remote(piece, piece, view_send.at[which], view_recv.at[which], {"view": pair}))
+        views_out[which].start()
+    total_loss = jnp.zeros((1, 1), F32)
+    for s in range(devices):
+        total_loss = total_loss + ret_in[0, s, body : body + 1, 0:1]
+    loss_out[...] = total_loss / (3.0 * height_px * width_px)
+    for copy in views_out:
+        copy.wait_recv()
+    for copy in cameras + records_out + grads_back + grads_across + views_out:
         copy.wait_send()
     left(goal_copies)
-    left(image_copies)
-
-
-def finish_kernel(sizes, params_ref, grads_ref, table_ref, picture_ref, grad_out, picture_out, flat):
+    for copies in image_copies:
+        left(copies)
+
+
+def finish_kernel(sizes, params_ref, grads_ref, table_ref, picture_ref, grad_hbm, picture_hbm, flat, grad_v, sems):
     views, splats, centre_x, centre_y = sizes
     param_rows = params_ref.shape[0]
     tall = splats // LANES
+    tiles = -(-param_rows // 8)
+    writes = [pltpu.make_async_copy(picture_ref, picture_hbm, sems.at[tiles])]
+    writes[0].start()
+
+    def write_tile(tile):
+        size = min(8, param_rows - 8 * tile)
+        for i in range(tall):
+            start = (tile * tall + i) * 8
+            grad_v[8 * tile : 8 * tile + size, i * LANES : (i + 1) * LANES] = flat[start : start + size, :]
+        rows = pl.ds(8 * tile, size)
+        writes.append(pltpu.make_async_copy(grad_v.at[rows], grad_hbm.at[rows], sems.at[tile]))
+        writes[-1].start()
+
     for tile in range(-(-param_rows // 8)):
         size = min(8, param_rows - 8 * tile)
         for i in range(tall) if tile < 2 else ():
@@ -796,9 +808,6 @@
     turns = [[[table_ref[v, r * 3 + c : r * 3 + c + 1, :] for c in range(3)] for r in range(3)] for v in range(views)]
     bases = [[table_ref[v, 9 + i : 10 + i, :] for i in range(16)] for v in range(views)]
     rows = [flat[place(i), :] for i in range(11)]
-    pull = jax.vjp(lambda r: geometry(r, turns, centre_x, centre_y), rows)[1]
-    for i, value in enumerate(pull([[grads_ref[v, f] for f in range(6)] for v in range(views)])[0]):
-        flat[place(i), :] = value
     for c in range(COLOURS):
         by_colour = [grads_ref[v, 6 + c] for v in range(views)]
         for i in range(16):
@@ -806,12 +815,15 @@
             for v in range(1, views):
                 value = value + bases[v][i] * by_colour[v]
             flat[place(11 + 3 * i + c), :] = value
-    for tile in range(-(-param_rows // 8)):
-        size = min(8, param_rows - 8 * tile)
-        for i in range(tall):
-            start = (tile * tall + i) * 8
-            grad_out[8 * tile : 8 * tile + size, i * LANES : (i + 1) * LANES] = flat[start : start + size, :]
-    picture_out[...] = picture_ref[...]
+    for tile in range(2, tiles):
+        write_tile(tile)
+    pull = jax.vjp(lambda r: geometry(r, turns, centre_x, centre_y), rows)[1]
+    for i, value in enumerate(pull([[grads_ref[v, f] for f in range(6)] for v in range(views)])[0]):
+        flat[place(i), :] = value
+    for tile in range(2):
+        write_tile(tile)
+    for copy in writes:
+        copy.wait()
 
 
 def shards(params, visible, blocks, counts, depth_rank, camera, background, target):
@@ -821,7 +833,7 @@
     strip_rows, width_px = target.shape[2:]
     splats = params.shape[1]
     tall = splats // LANES
-    subs = COLOURS * (width_px // LANES)
+    groups = width_px // LANES
     rows_in, rows_mid = strip_rows + 4 * HALO, strip_rows + 2 * HALO
     sizes = (devices, views, depth, slots, capacity, strip_rows, width_px, splats)
     per_tile = LANES // capacity
@@ -837,17 +849,17 @@
         vmem(-(-params.shape[0] // 8) * tall * 8, LANES), vmem(9, tall, LANES), pltpu.VMEM((2, depth, LANES), I32),
         vmem(8, LANES), vmem(views, 8, LANES),
         vmem(devices, message, LANES), vmem(devices, message, LANES),
-        vmem(devices, message, LANES), vmem(devices, message, LANES),
+        vmem(devices, message, LANES), vmem(2, devices, message, LANES),
         vmem(13, depth, LANES), half(6 * LANES, LANES), half(3 * LANES, 2 * LANES),
         half(3 * LANES, LANES), half(3 * LANES, LANES),
         half(6 * LANES, 2 * LANES), pltpu.VMEM((2 * tall, LANES), I32),
         vmem(depth, LANES, LANES), vmem(depth, LANES, LANES), vmem(5, LANES, LANES),
-        vmem(rows_in * subs, LANES), vmem(rows_in * subs, LANES),
-        vmem(3 * rows_mid * subs + 16, LANES), vmem(2 * rows_mid * subs, LANES), vmem(3 * rows_mid * subs, LANES),
-        vmem(3 * rows_mid * subs, LANES), vmem(rows_mid * subs, LANES), vmem(rows_mid * subs, LANES),
+        vmem(COLOURS, rows_in * groups, LANES), vmem(COLOURS, rows_in * groups, LANES),
+        vmem(6 * rows_mid * groups + 16, LANES), vmem(6 * rows_mid * groups, LANES), vmem(3 * rows_mid * groups, LANES),
+        vmem(3, rows_mid * groups, LANES), vmem(rows_mid * groups, LANES), vmem(rows_mid * groups, LANES),
         vmem(9, depth, LANES),
-        dma(8), dma(views), dma(views), dma(devices), dma(devices), dma(devices),
-        dma(devices), dma(2), dma(2), dma(2), dma(2), dma(9), dma(9),
+        dma(8), dma(views), dma(views), dma(devices), dma(devices), dma(2 * devices),
+        dma(2 * devices), dma(2), dma(2), dma(6), dma(6), dma(2), dma(2),
     ]
     whole = pl.BlockSpec(memory_space=pltpu.VMEM)
     grads, table, picture, loss = pl.pallas_call(
@@ -872,8 +884,10 @@
         name="finish",
         out_shape=(jax.ShapeDtypeStruct(params.shape, F32), jax.ShapeDtypeStruct(target.shape, F32)),
         in_specs=[whole] * 4,
-        out_specs=(whole,) * 2,
-        scratch_shapes=[vmem(-(-params.shape[0] // 8) * tall * 8, LANES)],
+        out_specs=(pl.BlockSpec(memory_space=pl.ANY),) * 2,
+        scratch_shapes=[
+            vmem(-(-params.shape[0] // 8) * tall * 8, LANES), vmem(*params.shape), dma(-(-params.shape[0] // 8) + 1)
+        ],
         compiler_params=pltpu.CompilerParams(vmem_limit_bytes=20 * 1024 * 1024),
     )(params, grads, table, picture)
     return (grad, picture, loss.reshape(1))

time: 33.5 us -> 32.1 us (0.958)
  Pallas kernels: 30.9 us -> 29.5 us
    pallas_call x1, Pallas kernels: 29.8 us -> 28.4 us  [shards(): pl.pallas_call(functools.partial(step_kernel, sizes), name='step', out_sh...]
where the time goes in v3:
time: 32.1 us; the launch traced here: 31.9 us
  Pallas kernels  29.5 us (92%)
  between operations  2.42 us (8%)
    pallas_call x1, Pallas kernels, shards(): pl.pallas_call(functools.partial(step_kernel, sizes), name='step', out_sh...  28.4 us
    pallas_call x1, Pallas kernels, shards(): pl.pallas_call(functools.partial(finish_kernel, (views, splats, *centre))...  1.11 us

profile of v3, /device:TPU:0, one launch (start us, length us, event | category | flops | bytes accessed | tf_op | source)
XLA Modules:
  0.0 31.9 jit_solution(6303968271578071931)
XLA Ops:
  0.6 0.0 copy-start
  0.6 28.4 %step.1 = (f32[4,9,16,128]{3,2,1,0:T(8,128)S(1)}, f32[4,32,128]{2,1,0:T(8,128)S(1)}, f32[1,3,16,512]{3,2,1,0:T(8,128)S(1)}, f32[1,1]{1,0:T(1,128)}) custom-call(f32[59,2048]{1,0:T(8,128)} %params_ref.1, s32[1,16,128]{2,1,0:T(8,128)} %bitcast.2, s32[1,128]{1,0:T(1,128)} %blocks_hbm.1, s32[1,8]{1,0:T(1,128)} %counts_hbm.1, s32[1,8]{1,0:T(1,128)} %rank_hbm.1, ...), custom_call_target="tpu_custom_call" | custom-call | tf_op jit(solution)/shard_map/step/pallas_call | solution.py:865
  29.0 0.0 copy-done
  29.0 1.1 %finish.1 = (f32[59,2048]{1,0:T(8,128)}, f32[1,3,16,512]{3,2,1,0:T(8,128)}) custom-call(f32[59,2048]{1,0:T(8,128)S(1)} %copy-done, f32[4,9,16,128]{3,2,1,0:T(8,128)S(1)} %get-tuple-element.9.grads_ref, f32[4,32,128]{2,1,0:T(8,128)S(1)} %get-tuple-element.10.table_ref, f32[1,3,16,512]{3,2,1,0:T(8,128)S(1)} %get-tuple-element.11.picture_ref), custom_call_target="tpu_custom_call" | custom-call | tf_op jit(solution)/shard_map/finish/pallas_call | solution.py:882
Async XLA Ops:
  0.6 28.4 %copy-start = (f32[59,2048]{1,0:T(8,128)S(1)}, f32[59,2048]{1,0:T(8,128)}, u32[]{:S(2)}) copy-start(f32[59,2048]{1,0:T(8,128)} %params_ref.1) | copy-start | bytes 1449988

commit v4 on v3

--- a/solution.py
+++ b/solution.py
@@ -177,7 +177,7 @@
     params_v, visible_v, blocks_v, counts_v, rank_v, camera_v, backdrop_v, target_v,
     flat, fields, lists, head, head_view, out_msg, in_msg, ret_out, ret_in,
     rec, place_f, place_b, nearer, further, taps_w, inverse, alpha_s, trans_s, seg, goal, image,
-    rows_buf, goal_buf, cols_buf, adj, seed_s, own_s, moments,
+    rows_buf, goal_buf, cols_buf, adj, seed_s, own_s, behind_s, spread,
     in_sem, camv_send, camv_recv, msg_send, msg_recv, ret_send, ret_recv,
     goal_send, goal_recv, image_send, image_recv, view_send, view_recv,
 ):
@@ -530,15 +530,16 @@
     across_lanes = iota(vreg, 1)
     to_natural = (across_lanes & 15) * 8 + lax.shift_right_logical(across_lanes, 4)
     from_natural = (across_lanes & 7) * 16 + lax.shift_right_logical(across_lanes, 3)
-    image_copies = []
+    image_copies, placed = [], []
     for ch in range(COLOURS):
         paired = jnp.concatenate(
             [jnp.concatenate([shares[ch][c], shares[ch][c + 8]], axis=1) for c in range(8)], axis=0
         )
-        placed = jnp.dot(
-            jnp.concatenate(three_parts(paired), axis=1), place_f[...], preferred_element_type=F32
+        placed.append(
+            jnp.dot(jnp.concatenate(three_parts(paired), axis=1), place_f[...], preferred_element_type=F32)
         )
-        for q, value in enumerate(swap_chunks([placed[c * 8 : c * 8 + 8] for c in range(8)], 8)):
+    for ch in range(COLOURS):
+        for q, value in enumerate(swap_chunks([placed[ch][c * 8 : c * 8 + 8] for c in range(8)], 8)):
             b, g = divmod(q, groups)
             value = jnp.take_along_axis(value, to_natural, axis=1, mode="promise_in_bounds") + backs[ch]
             image[ch, own_rows(b, g), :] = value
@@ -563,9 +564,9 @@
     def reader(ref, ch):
         return lambda at: ref[ch, at : at + 8, :]
 
-    def writer(base):
+    def writer(ch, base):
         def store(at, value):
-            rows_buf[8 + base + at : 16 + base + at, :] = value
+            rows_buf[ch, 8 + base + at : 16 + base + at, :] = value
 
         return store
 
@@ -574,12 +575,12 @@
     from_right = low_lanes & (sub_group < groups - 1)
     from_left = jnp.logical_not(low_lanes) & (sub_group > 0)
 
-    def blur_columns(first, size, terms):
+    def blur_columns(ch, first, size, terms):
         def read(at):
-            return rows_buf[at : at + size, :].reshape(size // 8, 8, LANES)
+            return rows_buf[ch, at : at + size, :].reshape(size // 8, 8, LANES)
 
         sides = jnp.where(from_right, read(first + 9), jnp.where(from_left, read(first + 7), 0.0))
-        own_parts = three_parts(rows_buf[first + 8 : first + 8 + size, :])[0:terms]
+        own_parts = three_parts(rows_buf[ch, first + 8 : first + 8 + size, :])[0:terms]
         rim_parts = three_parts(sides.reshape(size, LANES))[0:terms]
         both = jnp.dot(
             jnp.concatenate([v for pair in zip(own_parts, rim_parts) for v in pair], axis=1),
@@ -588,30 +589,31 @@
         )
         return (both[:, 0:LANES] + both[:, LANES : 2 * LANES]) * blur_norm
 
-    def blur_all(total, dst, terms=3):
+    def blur_all(ch, total, dst, terms=3):
         half = -(-total // 32) * 16
-        dst[0:half, :] = blur_columns(0, half, terms)
-        dst[half:total, :] = blur_columns(half, total - half, terms)
-
-    rows_buf[0:8, :] = jnp.zeros_like(rows_buf[0:8, :])
-    rows_buf[8 + 6 * mid : 16 + 6 * mid, :] = jnp.zeros_like(rows_buf[0:8, :])
+        dst[ch, 0:half, :] = blur_columns(ch, 0, half, terms)
+        dst[ch, half:total, :] = blur_columns(ch, half, total - half, terms)
+
+    for ch in range(COLOURS):
+        rows_buf[ch, 0:8, :] = jnp.zeros((8, LANES), F32)
+        rows_buf[ch, 8 + 3 * mid : 16 + 3 * mid, :] = jnp.zeros((8, LANES), F32)
     arrived(goal_copies)
     for ch in range(COLOURS):
         from_goal = reader(goal, ch)
-        blur_rows(from_goal, rows_mid, writer(2 * ch * mid))
-        blur_rows(lambda at: from_goal(at) * from_goal(at), rows_mid, writer((2 * ch + 1) * mid))
-    blur_all(6 * mid, goal_buf)
-
-    own_terms, pulled = None, []
-    for ch in range(COLOURS):
-        arrived(image_copies[ch])
+        blur_rows(from_goal, rows_mid, writer(ch, 0))
+        blur_rows(lambda at: from_goal(at) * from_goal(at), rows_mid, writer(ch, mid))
+        blur_all(ch, 2 * mid, goal_buf)
+
+    def blur_picture(ch):
         from_goal, from_image = reader(goal, ch), reader(image, ch)
-        blur_rows(from_image, rows_mid, writer(0))
-        blur_rows(lambda at: from_image(at) * from_image(at), rows_mid, writer(mid))
-        blur_rows(lambda at: from_image(at) * from_goal(at), rows_mid, writer(2 * mid))
-        blur_all(3 * mid, cols_buf)
-        mean_a, raw_aa, raw_ab = (cols_buf[q * mid : (q + 1) * mid, :] for q in range(3))
-        mean_b, raw_bb = (goal_buf[(2 * ch + q) * mid : (2 * ch + q + 1) * mid, :] for q in range(2))
+        blur_rows(from_image, rows_mid, writer(ch, 0))
+        blur_rows(lambda at: from_image(at) * from_image(at), rows_mid, writer(ch, mid))
+        blur_rows(lambda at: from_image(at) * from_goal(at), rows_mid, writer(ch, 2 * mid))
+        blur_all(ch, 3 * mid, cols_buf)
+
+    def terms_of(ch):
+        mean_a, raw_aa, raw_ab = (cols_buf[ch, q * mid : (q + 1) * mid, :] for q in range(3))
+        mean_b, raw_bb = (goal_buf[ch, q * mid : (q + 1) * mid, :] for q in range(2))
         centre_rows = slice(HALO * groups, HALO * groups + mid)
         pixel_a, pixel_b = image[ch, centre_rows, :], goal[ch, centre_rows, :]
         seed = seed_s[...]
@@ -626,36 +628,46 @@
         by_aa = -ssim * inv_second
         by_ab = 2.0 * first_n * scale
         by_a = 2.0 * (mean_b * second_n * scale - mean_a * (ssim * inv_first + by_aa)) - mean_b * by_ab
-        adj[0, 0:mid, :] = seed * by_a
-        adj[1, 0:mid, :] = seed * by_aa
-        adj[2, 0:mid, :] = seed * by_ab
+        adj[3 * ch, 0:mid, :] = seed * by_a
+        adj[3 * ch + 1, 0:mid, :] = seed * by_aa
+        adj[3 * ch + 2, 0:mid, :] = seed * by_ab
         differ = pixel_a - pixel_b
-        term = (0.8 * jnp.sqrt(differ * differ + SMOOTHING) + 0.2 * (1.0 - ssim)) * own_s[...]
-        own_terms = term if own_terms is None else own_terms + term
         for q in range(3):
-            blur_rows(reader(adj, q), strip_rows, writer(q * end))
-        blur_all(3 * end, cols_buf, terms=2)
+            blur_rows(reader(adj, 3 * ch + q), strip_rows, writer(ch, q * end))
+        blur_all(ch, 3 * end, cols_buf, terms=2)
+        return (0.8 * jnp.sqrt(differ * differ + SMOOTHING) + 0.2 * (1.0 - ssim)) * own_s[...]
+
+    def to_slots(ch):
         own_pixels = slice(MARGIN * groups, MARGIN * groups + end)
         pixel_a, pixel_b = image[ch, own_pixels, :], goal[ch, own_pixels, :]
         differ = pixel_a - pixel_b
-        adj[0, 0:end, :] = (
-            cols_buf[0:end, :]
-            + 2.0 * pixel_a * cols_buf[end : 2 * end, :]
-            + pixel_b * cols_buf[2 * end : 3 * end, :]
+        adj[3 * ch, 0:end, :] = (
+            cols_buf[ch, 0:end, :]
+            + 2.0 * pixel_a * cols_buf[ch, end : 2 * end, :]
+            + pixel_b * cols_buf[ch, 2 * end : 3 * end, :]
             + 0.8 * differ * lax.rsqrt(differ * differ + SMOOTHING)
         )
         bands_here = []
         for q in range(bands):
             b, g = divmod(q, groups)
-            value = adj[0, pl.ds(b * 8 * groups + g, 8, stride=groups), :]
+            value = adj[3 * ch, pl.ds(b * 8 * groups + g, 8, stride=groups), :]
             bands_here.append(jnp.take_along_axis(value, from_natural, axis=1, mode="promise_in_bounds"))
-        pulled.append(
-            jnp.dot(
-                jnp.concatenate(three_parts(jnp.concatenate(swap_chunks(bands_here, 8), axis=0)), axis=1),
-                place_b[...],
-                preferred_element_type=F32,
-            )
+        stacked = jnp.concatenate(swap_chunks(bands_here, 8), axis=0)
+        return jnp.dot(
+            jnp.concatenate(three_parts(stacked)[0:2], axis=1), place_b[0 : 2 * LANES, :], preferred_element_type=F32
         )
+
+    arrived(image_copies[0])
+    blur_picture(0)
+    arrived(image_copies[1])
+    blur_picture(1)
+    own_terms = terms_of(0)
+    arrived(image_copies[2])
+    blur_picture(2)
+    own_terms = own_terms + terms_of(1)
+    pulled = [to_slots(0)]
+    own_terms = own_terms + terms_of(2)
+    pulled += [to_slots(1), to_slots(2)]
     own_loss = jnp.sum(jnp.sum(own_terms, axis=1, keepdims=True), axis=0, keepdims=True)
 
     for c in range(16):
@@ -670,48 +682,54 @@
             seg[ch, part, :] = grad
             piece = grad * backs[ch]
             by_trans = piece if by_trans is None else by_trans + piece
-        rows_buf[part, :] = by_share * share
-        cols_buf[part, :] = by_trans
+        rows_buf[0, part, :] = by_share * share
+        behind_s[part, :] = by_trans
     by_log = jnp.dot(
-        jnp.concatenate(three_parts(rows_buf[0:LANES, :]), axis=1), further[...], preferred_element_type=F32
+        jnp.concatenate(three_parts(rows_buf[0, 0:LANES, :]), axis=1), further[...], preferred_element_type=F32
     )
     trans = seg[3]
     visible_through = trans > 2e-38
-    cols_buf[0:LANES, :] += jnp.where(visible_through, by_log / jnp.where(visible_through, trans, 1.0), 0.0)
+    behind_s[...] += jnp.where(visible_through, by_log / jnp.where(visible_through, trans, 1.0), 0.0)
 
     def unrender(step, carry):
-        k = depth - 1 - step
-        row = pl.ds(k, 1)
-
-        def across(f):
-            return jnp.broadcast_to(rec[f, row, :], vreg)
-
-        delta_y = across(1) + rows_f
-        first_x = across(0)
-        tint = [across(6 + ch) for ch in range(COLOURS)]
-        sums = [jnp.zeros(vreg, F32)] * 6
+        entries = [depth - 1 - 2 * step, depth - 2 - 2 * step]
+
+        def across(f, k):
+            return jnp.broadcast_to(rec[f, pl.ds(k, 1), :], vreg)
+
+        first_x = [across(0, k) for k in entries]
+        tint = [[across(6 + ch, k) for ch in range(COLOURS)] for k in entries]
+        sums = [[jnp.zeros(vreg, F32)] * 6 for _ in entries]
         for c in range(16):
             part = slice(c * 8, c * 8 + 8)
-            alpha = alpha_s[k, part, :]
-            weight = alpha * trans_s[k, part, :]
-            behind = cols_buf[part, :]
             grads = [seg[ch, part, :] for ch in range(COLOURS)]
-            gap = grads[0] * tint[0] + grads[1] * tint[1] + grads[2] * tint[2] - behind
-            cols_buf[part, :] = behind + alpha * gap
-            slope = weight * gap
-            delta_x = first_x + float(c)
-            slope_x = slope * delta_x
-            terms = [slope, slope_x, slope_x * delta_x] + [weight * g for g in grads]
-            sums = [a + b for a, b in zip(sums, terms)]
-        rows = [
-            sums[0], sums[1], sums[0] * delta_y, sums[2], sums[1] * delta_y, sums[0] * delta_y * delta_y,
-            sums[3], sums[4], sums[5],
-        ]
-        for f, value in enumerate(rows):
-            moments[f, row, :] = jnp.sum(value, axis=0, keepdims=True)
+            behind = behind_s[part, :]
+            for n, k in enumerate(entries):
+                alpha = alpha_s[k, part, :]
+                weight = alpha * trans_s[k, part, :]
+                gap = grads[0] * tint[n][0] + grads[1] * tint[n][1] + grads[2] * tint[n][2] - behind
+                behind = behind + alpha * gap
+                slope = weight * gap
+                delta_x = first_x[n] + float(c)
+                slope_x = slope * delta_x
+                terms = [slope, slope_x, slope_x * delta_x] + [weight * g for g in grads]
+                sums[n] = [a + b for a, b in zip(sums[n], terms)]
+            behind_s[part, :] = behind
+        for n, k in enumerate(entries):
+            delta_y = across(1, k) + rows_f
+            by_y, total = sums[n][0] * delta_y, sums[n]
+            rows = [total[0], total[1], by_y, total[2], total[1] * delta_y, by_y * delta_y, *total[3:6]]
+            for f, value in enumerate(rows):
+                spread[f, pl.ds(pl.multiple_of(k * 8, 8), 8), :] = value
         return carry
 
-    lax.fori_loop(0, depth, unrender, 0)
+    lax.fori_loop(0, depth // 2, unrender, 0)
+    moments = []
+    for f in range(9):
+        total = spread[f, pl.ds(0, depth, stride=8), :]
+        for r in range(1, 8):
+            total = total + spread[f, pl.ds(r, depth, stride=8), :]
+        moments.append(total)
     conic_a, conic_b, conic_c, opaque = [rec[9 + i] for i in range(4)]
     grads_out = [
         conic_a * moments[1] + conic_b * moments[2],
@@ -855,9 +873,9 @@
         half(6 * LANES, 2 * LANES), pltpu.VMEM((2 * tall, LANES), I32),
         vmem(depth, LANES, LANES), vmem(depth, LANES, LANES), vmem(5, LANES, LANES),
         vmem(COLOURS, rows_in * groups, LANES), vmem(COLOURS, rows_in * groups, LANES),
-        vmem(6 * rows_mid * groups + 16, LANES), vmem(6 * rows_mid * groups, LANES), vmem(3 * rows_mid * groups, LANES),
-        vmem(3, rows_mid * groups, LANES), vmem(rows_mid * groups, LANES), vmem(rows_mid * groups, LANES),
-        vmem(9, depth, LANES),
+        vmem(COLOURS, 3 * rows_mid * groups + 16, LANES), vmem(COLOURS, 2 * rows_mid * groups, LANES),
+        vmem(COLOURS, 3 * rows_mid * groups, LANES), vmem(3 * COLOURS, rows_mid * groups, LANES),
+        vmem(rows_mid * groups, LANES), vmem(rows_mid * groups, LANES), vmem(LANES, LANES), vmem(9, 8 * depth, LANES),
         dma(8), dma(views), dma(views), dma(devices), dma(devices), dma(2 * devices),
         dma(2 * devices), dma(2), dma(2), dma(6), dma(6), dma(2), dma(2),
     ]

time: 32.1 us -> 30.9 us (0.963)
  Pallas kernels: 29.5 us -> 28.3 us
    pallas_call x1, Pallas kernels: 28.4 us -> 27.2 us  [shards(): pl.pallas_call(functools.partial(step_kernel, sizes), name='step', out_sh...]
where the time goes in v4:
time: 30.9 us; the launch traced here: 30.7 us
  Pallas kernels  28.3 us (92%)
  between operations  2.42 us (8%)
    pallas_call x1, Pallas kernels, shards(): pl.pallas_call(functools.partial(step_kernel, sizes), name='step', out_sh...  27.2 us
    pallas_call x1, Pallas kernels, shards(): pl.pallas_call(functools.partial(finish_kernel, (views, splats, *centre))...  1.11 us

profile of v4, /device:TPU:0, one launch (start us, length us, event | category | flops | bytes accessed | tf_op | source)
XLA Modules:
  0.0 30.7 jit_solution(15218839126979744864)
XLA Ops:
  0.6 0.0 copy-start
  0.6 27.2 %step.1 = (f32[4,9,16,128]{3,2,1,0:T(8,128)S(1)}, f32[4,32,128]{2,1,0:T(8,128)S(1)}, f32[1,3,16,512]{3,2,1,0:T(8,128)S(1)}, f32[1,1]{1,0:T(1,128)}) custom-call(f32[59,2048]{1,0:T(8,128)} %params_ref.1, s32[1,16,128]{2,1,0:T(8,128)} %bitcast.2, s32[1,128]{1,0:T(1,128)} %blocks_hbm.1, s32[1,8]{1,0:T(1,128)} %counts_hbm.1, s32[1,8]{1,0:T(1,128)} %rank_hbm.1, ...), custom_call_target="tpu_custom_call" | custom-call | tf_op jit(solution)/shard_map/step/pallas_call | solution.py:883
  27.8 0.0 copy-done
  27.8 1.1 %finish.1 = (f32[59,2048]{1,0:T(8,128)}, f32[1,3,16,512]{3,2,1,0:T(8,128)}) custom-call(f32[59,2048]{1,0:T(8,128)S(1)} %copy-done, f32[4,9,16,128]{3,2,1,0:T(8,128)S(1)} %get-tuple-element.9.grads_ref, f32[4,32,128]{2,1,0:T(8,128)S(1)} %get-tuple-element.10.table_ref, f32[1,3,16,512]{3,2,1,0:T(8,128)S(1)} %get-tuple-element.11.picture_ref), custom_call_target="tpu_custom_call" | custom-call | tf_op jit(solution)/shard_map/finish/pallas_call | solution.py:900
Async XLA Ops:
  0.6 27.2 %copy-start = (f32[59,2048]{1,0:T(8,128)S(1)}, f32[59,2048]{1,0:T(8,128)}, u32[]{:S(2)}) copy-start(f32[59,2048]{1,0:T(8,128)} %params_ref.1) | copy-start | bytes 1449988

commit v5 on v4

--- a/solution.py
+++ b/solution.py
@@ -176,8 +176,8 @@
     view_grads, table_out, picture_out, loss_out,
     params_v, visible_v, blocks_v, counts_v, rank_v, camera_v, backdrop_v, target_v,
     flat, fields, lists, head, head_view, out_msg, in_msg, ret_out, ret_in,
-    rec, place_f, place_b, nearer, further, taps_w, inverse, alpha_s, trans_s, seg, goal, image,
-    rows_buf, goal_buf, cols_buf, adj, seed_s, own_s, behind_s, spread,
+    rec, place_f, place_b, nearer, further, taps_w, inverse, alpha_s, weight_s, seg, goal, image,
+    rows_buf, goal_buf, cols_buf, adj, seed_s, own_s, behind_s, spread, ahead_s,
     in_sem, camv_send, camv_recv, msg_send, msg_recv, ret_send, ret_recv,
     goal_send, goal_recv, image_send, image_recv, view_send, view_recv,
 ):
@@ -206,11 +206,13 @@
     for target in greeted:
         pl.semaphore_signal(barrier, inc=1, device_id=target, device_id_type=pl.DeviceIdType.MESH)
     pairs = [
-        (blocks_hbm, blocks_v), (counts_hbm, counts_v), (camera_hbm, camera_v), (params_hbm, params_v),
+        (blocks_hbm, blocks_v), (counts_hbm, counts_v), (camera_hbm, camera_v),
+        (params_hbm.at[pl.ds(0, 16)], params_v.at[pl.ds(0, 16)]),
         (visible_hbm.at[0], visible_v), (rank_hbm, rank_v), (backdrop_hbm, backdrop_v), (target_hbm.at[0], target_v),
+        (params_hbm.at[pl.ds(16, param_rows - 16)], params_v.at[pl.ds(16, param_rows - 16)]),
     ]
     fetches = [pltpu.make_async_copy(a, b, in_sem.at[i]) for i, (a, b) in enumerate(pairs)]
-    for fetch in fetches:
+    for fetch in fetches[3:4] + fetches[8:9] + fetches[0:3] + fetches[4:8]:
         fetch.start()
 
     rim = MARGIN * groups
@@ -245,12 +247,15 @@
             device_id_type=pl.DeviceIdType.MESH,
         )
 
+    def flatten(tiles):
+        for tile in tiles:
+            size = min(8, param_rows - 8 * tile)
+            for i in range(tall):
+                start = (tile * tall + i) * 8
+                flat[start : start + size, :] = params_v[8 * tile : 8 * tile + size, i * LANES : (i + 1) * LANES]
+
     fetches[3].wait()
-    for tile in range(-(-param_rows // 8)):
-        size = min(8, param_rows - 8 * tile)
-        for i in range(tall):
-            start = (tile * tall + i) * 8
-            flat[start : start + size, :] = params_v[8 * tile : 8 * tile + size, i * LANES : (i + 1) * LANES]
+    flatten(range(2))
 
     def param_row(row):
         return flat[pl.ds(row // 8 * tall * 8 + row % 8, tall, stride=8), :]
@@ -261,6 +266,8 @@
     turn = turn_of(camera_v[...])
     record = geometry([param_row(i) for i in range(11)], [turn], centre_x, centre_y)[0]
     basis = harmonics(turn[2])
+    fetches[8].wait()
+    flatten(range(2, -(-param_rows // 8)))
     for c in range(COLOURS):
         colour = 0.5 + basis[0] * param_row(11 + c)
         for i in range(1, 16):
@@ -401,6 +408,11 @@
                 start = (term * 2 + part) * LANES
                 taps_w[start : start + LANES, side * LANES : (side + 1) * LANES] = weights
 
+    ranks_f = ranks.astype(F32)
+    diagonal = iota(square, 0) == iota(square, 1)
+    ranks_c = jnp.sum(jnp.where(diagonal, ranks_f, 0.0), axis=1, keepdims=True)
+    ahead_s[0] = jnp.where(ranks_c < ranks_f, 1.0, 0.0)
+    ahead_s[1] = jnp.where(ranks_c > ranks_f, 1.0, 0.0)
     slot_value = lane.astype(F32)
 
     def invert(k, total):
@@ -473,8 +485,8 @@
                 alpha = jnp.exp2((curve * delta_x + cross) * delta_x + square_y)
                 place = pl.ds(pl.multiple_of((index * width_c + j) * 8, 8), 8)
                 alpha_s[k, place, :] = alpha
-                trans_s[k, place, :] = trans[j]
                 weight = alpha * trans[j]
+                weight_s[k, place, :] = weight
                 for ch in range(COLOURS):
                     sums[ch][j] = sums[ch][j] + weight * tint[ch]
                 kept = 1.0 - alpha
@@ -492,13 +504,10 @@
 
     lax.fori_loop(0, 16 // width_c, render_some, 0)
 
-    diagonal = iota(square, 0) == iota(square, 1)
-    ranks_f = ranks.astype(F32)
-    owned_c = jnp.sum(jnp.where(diagonal, owned, 0.0), axis=1, keepdims=True)
-    ranks_c = jnp.sum(jnp.where(diagonal, ranks_f, 0.0), axis=1, keepdims=True)
+    owned_c = jnp.transpose(jnp.broadcast_to(owned, (8, LANES)))[:, 0:1]
     same = owned_c == owned
-    fwd_mask = jnp.where(same & (ranks_c < ranks_f), 1.0, 0.0).astype(BF16)
-    bwd_mask = jnp.where(same & (ranks_c > ranks_f), 1.0, 0.0).astype(BF16)
+    fwd_mask = jnp.where(same, ahead_s[0], 0.0).astype(BF16)
+    bwd_mask = jnp.where(same, ahead_s[1], 0.0).astype(BF16)
     blocks_here = LANES // 2
     lane_sq, sub_sq = iota(square, 1).astype(F32), iota(square, 0).astype(F32)
     for part in range(3):
@@ -508,7 +517,7 @@
         alive = owned_c >= 0.0
         forth = jnp.where(alive & (lane_sq == owned_c + d * blocks_here), 1.0, 0.0).astype(BF16)
         back = jnp.where((owned >= 0.0) & (sub_sq == owned + d * blocks_here), 1.0, 0.0).astype(BF16)
-        for part in range(3):
+        for part in range(2):
             place_f[(part * 2 + d) * LANES : (part * 2 + d + 1) * LANES, :] = forth
             place_b[part * LANES : (part + 1) * LANES, d * LANES : (d + 1) * LANES] = back
 
@@ -536,7 +545,9 @@
             [jnp.concatenate([shares[ch][c], shares[ch][c + 8]], axis=1) for c in range(8)], axis=0
         )
         placed.append(
-            jnp.dot(jnp.concatenate(three_parts(paired), axis=1), place_f[...], preferred_element_type=F32)
+            jnp.dot(
+                jnp.concatenate(three_parts(paired)[0:2], axis=1), place_f[0 : 4 * LANES, :], preferred_element_type=F32
+            )
         )
     for ch in range(COLOURS):
         for q, value in enumerate(swap_chunks([placed[ch][c * 8 : c * 8 + 8] for c in range(8)], 8)):
@@ -706,7 +717,7 @@
             behind = behind_s[part, :]
             for n, k in enumerate(entries):
                 alpha = alpha_s[k, part, :]
-                weight = alpha * trans_s[k, part, :]
+                weight = weight_s[k, part, :]
                 gap = grads[0] * tint[n][0] + grads[1] * tint[n][1] + grads[2] * tint[n][2] - behind
                 behind = behind + alpha * gap
                 slope = weight * gap
@@ -754,7 +765,7 @@
         )
         for d, peer in enumerate(peers + [me])
     ]
-    for copy in grads_across + grads_back:
+    for copy in grads_back + grads_across:
         copy.start()
     ret_in[0, me] = ret_out[me]
 
@@ -766,10 +777,10 @@
             table_out[v, i : i + 1, :] = jnp.broadcast_to(value, (1, LANES))
 
     views_out = []
-    for which, (view, waits) in enumerate(((across_x, grads_across), (my_view, grads_back))):
+    for which, (view, waits) in enumerate(((my_view, grads_back), (across_x, grads_across))):
         for copy in waits:
             copy.wait_recv()
-        for f, value in enumerate(unpack(ret_in.at[1 - which])):
+        for f, value in enumerate(unpack(ret_in.at[which])):
             fields[f] = value
         for half in range(tall // 8):
             slot_of = inverse[half * 8 : half * 8 + 8, :]
@@ -876,7 +887,8 @@
         vmem(COLOURS, 3 * rows_mid * groups + 16, LANES), vmem(COLOURS, 2 * rows_mid * groups, LANES),
         vmem(COLOURS, 3 * rows_mid * groups, LANES), vmem(3 * COLOURS, rows_mid * groups, LANES),
         vmem(rows_mid * groups, LANES), vmem(rows_mid * groups, LANES), vmem(LANES, LANES), vmem(9, 8 * depth, LANES),
-        dma(8), dma(views), dma(views), dma(devices), dma(devices), dma(2 * devices),
+        vmem(2, LANES, LANES),
+        dma(9), dma(views), dma(views), dma(devices), dma(devices), dma(2 * devices),
         dma(2 * devices), dma(2), dma(2), dma(6), dma(6), dma(2), dma(2),
     ]
     whole = pl.BlockSpec(memory_space=pltpu.VMEM)

time: 30.9 us -> 30.9 us (level)
  no operation moved by 1% of the time
where the time goes in v5:
time: 30.9 us; the launch traced here: 30.8 us
  Pallas kernels  28.3 us (92%)
  between operations  2.42 us (8%)
    pallas_call x1, Pallas kernels, shards(): pl.pallas_call(functools.partial(step_kernel, sizes), name='step', out_sh...  27.2 us
    pallas_call x1, Pallas kernels, shards(): pl.pallas_call(functools.partial(finish_kernel, (views, splats, *centre))...  1.11 us

profile of v5, /device:TPU:0, one launch (start us, length us, event | category | flops | bytes accessed | tf_op | source)
XLA Modules:
  0.0 30.8 jit_solution(8029948741018931278)
XLA Ops:
  0.6 0.0 copy-start
  0.6 27.2 %step.1 = (f32[4,9,16,128]{3,2,1,0:T(8,128)S(1)}, f32[4,32,128]{2,1,0:T(8,128)S(1)}, f32[1,3,16,512]{3,2,1,0:T(8,128)S(1)}, f32[1,1]{1,0:T(1,128)}) custom-call(f32[59,2048]{1,0:T(8,128)} %params_ref.1, s32[1,16,128]{2,1,0:T(8,128)} %bitcast.2, s32[1,128]{1,0:T(1,128)} %blocks_hbm.1, s32[1,8]{1,0:T(1,128)} %counts_hbm.1, s32[1,8]{1,0:T(1,128)} %rank_hbm.1, ...), custom_call_target="tpu_custom_call" | custom-call | tf_op jit(solution)/shard_map/step/pallas_call | solution.py:895
  27.9 0.0 copy-done
  27.9 1.1 %finish.1 = (f32[59,2048]{1,0:T(8,128)}, f32[1,3,16,512]{3,2,1,0:T(8,128)}) custom-call(f32[59,2048]{1,0:T(8,128)S(1)} %copy-done, f32[4,9,16,128]{3,2,1,0:T(8,128)S(1)} %get-tuple-element.9.grads_ref, f32[4,32,128]{2,1,0:T(8,128)S(1)} %get-tuple-element.10.table_ref, f32[1,3,16,512]{3,2,1,0:T(8,128)S(1)} %get-tuple-element.11.picture_ref), custom_call_target="tpu_custom_call" | custom-call | tf_op jit(solution)/shard_map/finish/pallas_call | solution.py:912
Async XLA Ops:
  0.6 27.2 %copy-start = (f32[59,2048]{1,0:T(8,128)S(1)}, f32[59,2048]{1,0:T(8,128)}, u32[]{:S(2)}) copy-start(f32[59,2048]{1,0:T(8,128)} %params_ref.1) | copy-start | bytes 1449988
